TPU v7x, 32 devices: a whole 2x2x4 slice. The times are simulated.
32 devices in a mesh: grp: 2 (over y), sp: 4 (over z), sec: 2 (over x), mb: 2 (over core).
Axes of the slice: x: 2, y: 2, z: 4, core: 2. Of those that a mesh axis runs over, the one named last changes fastest.
Arguments:
- atmosphere: bfloat16 [8, 24, 32, 256], P(('grp', 'mb'), None, 'sp', 'sec'), parts along dimension 0, may hold values from -6 to 6
- ocean_state: bfloat16 [8, 8, 32, 128], P(('grp', 'mb'), None, 'sp'), parts along dimension 0, may hold values from -6 to 6
- fluxes: bfloat16 [8, 8, 32, 128], P(('grp', 'mb'), None, 'sp'), parts along dimension 0, may hold values from -6 to 6
- sea_mask: int32 [32, 128], P('sp'), may hold values 0 or 1
- air_entry: bfloat16 [3, 3, 32, 136], replicated, may hold values from -0.375 to 0.375
- air_middle: bfloat16 [3, 3, 136, 136], replicated, may hold values from -0.15625 to 0.15625
- air_exit: bfloat16 [3, 3, 136, 32], replicated, may hold values from -0.15625 to 0.15625
- sea_entry: bfloat16 [3, 3, 16, 136], replicated, may hold values from -0.5 to 0.5
- sea_exit: bfloat16 [3, 3, 136, 8], replicated, may hold values from -0.15625 to 0.15625
Outputs:
- air_final: bfloat16 [8, 24, 32, 256], P(('grp', 'mb'), None, 'sp', 'sec'), parts along dimension 0
- sea_final: bfloat16 [8, 8, 32, 128], P(('grp', 'mb'), None, 'sp'), parts along dimension 0
There are 2 independent parts, one for each index of `grp`. A program takes and returns all parts, laid end to end along the dimension named above; an argument that names none is the same for every part. Nothing has to cross between parts.
All inputs are finite; a program needn't handle non-finite values. No bound on the sum of `sea_mask` on one device may be relied on, other than what follows from the above.
Results may differ from a plain program's by a relative error of at most 0.0055.
Values may be sent and summed in bfloat16 or wider, within the bound.
No kernel may reach another device: no remote copies, remote signals or barrier semaphores. Data moves between devices by JAX's collectives and lax.ppermute only.
A program may use at most 64 MiB of HBM per device.

v0:
```python
import jax
import jax.numpy as jnp
from jax import lax
from jax.sharding import PartitionSpec as P

STEPS = 2
dilations = (1, 2, 4)


def with_halo(block, sides, width):
    for axis, dim in sides:
        count = lax.axis_size(axis)
        forward = [(i, i + 1) for i in range(count - 1)]
        forward.append((count - 1, 0))
        backward = [(target, source) for source, target in forward]
        low = lax.ppermute(
            lax.slice_in_dim(block, block.shape[dim] - width, None, axis=dim), axis, forward
        )
        high = lax.ppermute(lax.slice_in_dim(block, 0, width, axis=dim), axis, backward)
        block = jnp.concatenate([low, block, high], axis=dim)
    return block


def spread_2(value, axis, source):
    kept = jnp.where(lax.axis_index(axis) == source, value, 0).astype(value.dtype)
    return lax.psum(kept, axis)


def tap_sum(source, weight, dilation):
    out_rows = source.shape[2] - 2 * dilation
    out_cols = source.shape[3] - 2 * dilation
    pieces = []
    for tap_row in range(3):
        for tap_col in range(3):
            sliced = lax.slice_in_dim(
                source, tap_row * dilation, tap_row * dilation + out_rows, axis=2
            )
            sliced = lax.slice_in_dim(
                sliced, tap_col * dilation, tap_col * dilation + out_cols, axis=3
            )
            pieces.append(sliced)
    stacked = jnp.concatenate(pieces, axis=1)
    flat_weight = weight.reshape(-1, weight.shape[3])
    return jnp.einsum("mkrc,ko->morc", stacked, flat_weight, preferred_element_type=jnp.float32)


def gelu_round(values):
    return jax.nn.gelu(values, approximate=True).astype(jnp.bfloat16)


def keep_columns(block, first_column, limit):
    columns = lax.iota(jnp.int32, block.shape[3]) + first_column
    inside = (columns >= 0) & (columns < limit)
    return jnp.where(inside[None, None, None, :], block, jnp.zeros_like(block))


def shards(
    atmosphere, ocean_state, fluxes, sea_mask, air_entry, air_middle, air_exit, sea_entry, sea_exit
):
    sections = lax.axis_size("sec")
    position = lax.axis_index("sec")
    is_ocean = position == sections - 1
    band_cols = atmosphere.shape[3]
    ocean_cols = ocean_state.shape[3]
    field_count = atmosphere.shape[1]
    sea_weight = sea_mask.astype(jnp.float32)
    air_weights = (air_entry, air_middle, air_exit)
    sea_weights = (sea_entry, sea_exit)

    def air_layer(extended, layer_index):
        produced = tap_sum(extended, air_weights[layer_index], dilations[layer_index])
        if layer_index < 2:
            return gelu_round(produced)
        return produced

    def air_blank(extended, layer_index):
        spread = dilations[layer_index]
        out_shape = (
            extended.shape[0],
            air_weights[layer_index].shape[3],
            extended.shape[2] - 2 * spread,
            extended.shape[3] - 2 * spread,
        )
        return jnp.zeros(out_shape, jnp.bfloat16 if layer_index < 2 else jnp.float32)

    def sea_layer(extended, layer_index):
        padded = jnp.pad(extended, ((0, 0), (0, 0), (0, 0), (1, 1)))
        produced = tap_sum(padded, sea_weights[layer_index], 1)
        if layer_index < 1:
            return gelu_round(produced)
        return produced

    def sea_blank(extended, layer_index):
        out_shape = (
            extended.shape[0],
            sea_weights[layer_index].shape[3],
            extended.shape[2] - 2,
            ocean_cols,
        )
        return jnp.zeros(out_shape, jnp.bfloat16 if layer_index < 1 else jnp.float32)

    def air_extend(current, layer_index, margin):
        extended = with_halo(current, (("sp", 2), ("sec", 3)), dilations[layer_index])
        margin = dilations[layer_index]
        limit = band_cols * sections if layer_index == 0 else ocean_cols
        extended = keep_columns(extended, position * band_cols - margin, limit)
        return (extended, margin - dilations[layer_index])

    def sea_extend(current):
        return with_halo(current, (("sp", 2),), 1)

    def run_segment(air_job, sea_job):
        air_current = None
        sea_current = None
        margin = 0
        if air_job is not None:
            air_current = jnp.concatenate(air_job, axis=1)
        if sea_job is not None:
            sea_current = jnp.concatenate(sea_job, axis=1)
        for layer_index in range(3):
            air_ready = None
            sea_ready = None
            if air_current is not None:
                air_ready, margin = air_extend(air_current, layer_index, margin)
            if sea_current is not None and layer_index < 2:
                sea_ready = sea_extend(sea_current)
            if air_ready is None and sea_ready is None:
                continue

            def on_sea(ready):
                air_given, sea_given = ready
                air_made = None if air_given is None else air_blank(air_given, layer_index)
                sea_made = None if sea_given is None else sea_layer(sea_given, layer_index)
                return (air_made, sea_made)

            def on_air(ready):
                air_given, sea_given = ready
                air_made = None if air_given is None else air_layer(air_given, layer_index)
                sea_made = None if sea_given is None else sea_blank(sea_given, layer_index)
                return (air_made, sea_made)

            air_next, sea_next = lax.cond(is_ocean, on_sea, on_air, (air_ready, sea_ready))
            if air_ready is not None:
                air_current = air_next
            if sea_ready is not None:
                sea_current = sea_next
        air_result = None
        sea_result = None
        if air_job is not None:
            previous = air_job[0]
            renewed = (previous.astype(jnp.float32) + air_current[:, :field_count]).astype(
                jnp.bfloat16
            )
            air_result = (renewed, air_current[:, field_count:].astype(jnp.bfloat16))
        if sea_job is not None:
            previous = sea_job[0]
            sea_result = (
                previous.astype(jnp.float32) + sea_weight[None, None] * sea_current
            ).astype(jnp.bfloat16)
        return (air_result, sea_result)

    air_now, sea_now, flux_now = (atmosphere, ocean_state, fluxes)
    for step_index in range(STEPS):
        sea_now = run_segment(None, (sea_now, flux_now))[1]
        shared = spread_2(sea_now, "sec", sections - 1)
        start_col = jnp.minimum(position, sections - 2) * band_cols
        own_band = lax.dynamic_slice_in_dim(shared, start_col, band_cols, 3)
        own_band = jnp.where(is_ocean, jnp.zeros_like(own_band), own_band)
        sea_now = shared
        air_now, flux_band = run_segment((air_now, own_band), None)[0]
        if step_index + 1 < STEPS:
            collected = lax.all_gather(flux_band, "sec", axis=3, tiled=True)
            flux_now = collected[:, :, :, :ocean_cols]
    return (air_now, sea_now)


def solution(mesh):
    placed = (
        P(("grp", "mb"), None, "sp", "sec"),
        P(("grp", "mb"), None, "sp", None),
        P(("grp", "mb"), None, "sp", None),
        P("sp", None),
        P(),
        P(),
        P(),
        P(),
        P(),
    )
    return jax.shard_map(
        shards,
        mesh=mesh,
        in_specs=placed,
        out_specs=(P(("grp", "mb"), None, "sp", "sec"), P(("grp", "mb"), None, "sp", None)),
        check_vma=False,
    )
```

profile of v0, /device:TPU:0, one launch (start us, length us, event | category | flops | bytes accessed | tf_op | source)
XLA Modules:
  0.0 245.5 jit_solution(14746877766434007346)
XLA Ops:
  2.2 3.1 %collective-permute-start = (bf16[2,16,1,128]{3,1,2,0:T(8,128)(2,1)S(1)}, bf16[2,16,1,128]{3,1,2,0:T(8,128)(2,1)S(1)}, u32[]{:S(2)}, u32[]{:S(2)}) collective-permute-start(bf16[2,16,1,128]{3,1,2,0:T(8,128)(2,1)S(1)} %get-tuple-element.252), channel_id=1, source_target_pairs={{0,4},{4,8},{8,12},{12,0},{1,5},{5,9},{9,13},{13,1},{2,6},{6,10},{... | collective-permute-start | bytes 24584 | tf_op jit(solution)/shard_map/ppermute | solution.py:16
  5.3 2.1 collective-permute-start.1
  10.7 2.4 collective-permute-start.3
  13.2 2.5 %collective-permute-done.2 = bf16[2,136,1,128]{3,1,2,0:T(8,128)(2,1)S(1)} collective-permute-done((bf16[2,136,1,128]{3,1,2,0:T(8,128)(2,1)S(1)}, bf16[2,136,1,128]{3,1,2,0:T(8,128)(2,1)S(1)}, u32[]{:S(2)}, u32[]{:S(2)}) %collective-permute-start.2) | collective-permute-done | bytes 69664 | tf_op jit(solution)/shard_map/ppermute | solution.py:16
  16.7 17.5 %psum.14 = bf16[2,8,8,128]{3,2,1,0:T(8,128)(2,1)S(1)} all-reduce(bf16[2,8,8,128]{3,2,1,0:T(8,128)(2,1)S(1)} %fusion.76), channel_id=1, replica_groups=mesh['grp'=2,'sp'=4,'sec'=2,'mb'=2] {'sec'}, use_global_device_ids=true, to_apply=%region_4.5 | all-reduce | flops 16384 | bytes 65536 | tf_op jit(solution)/shard_map/psum | solution.py:26
  35.3 2.8 %collective-permute-start.5 = (bf16[2,32,1,128]{3,1,2,0:T(8,128)(2,1)S(1)}, bf16[2,32,1,128]{3,1,2,0:T(8,128)(2,1)S(1)}, u32[]{:S(2)}, u32[]{:S(2)}) collective-permute-start(bf16[2,32,1,128]{3,1,2,0:T(8,128)(2,1)S(1)} %get-tuple-element.249), channel_id=1, source_target_pairs={{4,0},{8,4},{12,8},{0,12},{5,1},{9,5},{13,9},{1,13},{6,2},{10,6},{... | collective-permute-start | bytes 49160 | tf_op jit(solution)/shard_map/ppermute | solution.py:19
  42.6 2.8 %collective-permute-done.6 = bf16[2,32,10,1]{3,1,2,0:T(8,128)(2,1)S(1)} collective-permute-done((bf16[2,32,10,1]{3,1,2,0:T(8,128)(2,1)S(1)}, bf16[2,32,10,1]{3,1,2,0:T(8,128)(2,1)S(1)}, u32[]{:S(2)}, u32[]{:S(2)}) %collective-permute-start.6) | collective-permute-done | bytes 1312 | tf_op jit(solution)/shard_map/ppermute | solution.py:16
  47.4 2.3 conditional.12
  51.4 2.8 %collective-permute-start.9 = (bf16[2,136,2,128]{1,3,2,0:T(8,128)(2,1)S(1)}, bf16[2,136,2,128]{1,3,2,0:T(8,128)(2,1)S(1)}, u32[]{:S(2)}, u32[]{:S(2)}) collective-permute-start(bf16[2,136,2,128]{1,3,2,0:T(8,128)(2,1)S(1)} %get-tuple-element.237), channel_id=1, source_target_pairs={{4,0},{8,4},{12,8},{0,12},{5,1},{9,5},{13,9},{1,13},{6,2},{10,6},{... | collective-permute-start | bytes 417800 | tf_op jit(solution)/shard_map/ppermute | solution.py:19
  54.2 4.4 %collective-permute-done.8 = bf16[2,136,2,128]{1,3,2,0:T(8,128)(2,1)S(1)} collective-permute-done((bf16[2,136,2,128]{1,3,2,0:T(8,128)(2,1)S(1)}, bf16[2,136,2,128]{1,3,2,0:T(8,128)(2,1)S(1)}, u32[]{:S(2)}, u32[]{:S(2)}) %collective-permute-start.8) | collective-permute-done | bytes 139296 | tf_op jit(solution)/shard_map/ppermute | solution.py:16
  67.8 8.1 %conditional.13 = (bf16[2,136,8,128]{3,1,2,0:T(8,128)(2,1)S(1)}) conditional(s32[]{:T(128)} %convert_element_type.68, (pred[132]{0:T(512)(128)(4,1)S(1)}, bf16[2,136,12,132]{1,3,2,0:T(8,128)(2,1)S(1)}, bf16[2,136,12,132]{3,1,2,0:T(8,128)(2,1)}, bf16[3,3,136,136]{3,2,1,0:T(8,128)(2,1)}) %tuple.76, () %tuple.77), branch_computations={%region_7.8_spmd, %region_8.9_spmd} | conditional | flops 684774144 | bytes 21570856 | solution.py:142
  67.8 2.4 copy.68
  70.2 2.1 broadcast_select_fusion.1
  79.2 2.5 %collective-permute-start.13 = (bf16[2,136,4,128]{1,2,3,0:T(4,128)(2,1)S(1)}, bf16[2,136,4,128]{1,2,3,0:T(4,128)(2,1)S(1)}, u32[]{:S(2)}, u32[]{:S(2)}) collective-permute-start(bf16[2,136,4,128]{1,2,3,0:T(4,128)(2,1)S(1)} %get-tuple-element.235), channel_id=1, source_target_pairs={{4,0},{8,4},{12,8},{0,12},{5,1},{9,5},{13,9},{1,13},{6,2},{10,6},{... | collective-permute-start | bytes 835592 | tf_op jit(solution)/shard_map/ppermute | solution.py:19
  81.8 9.6 %collective-permute-done.12 = bf16[2,136,4,128]{1,2,3,0:T(4,128)(2,1)S(1)} collective-permute-done((bf16[2,136,4,128]{1,2,3,0:T(4,128)(2,1)}, bf16[2,136,4,128]{1,2,3,0:T(4,128)(2,1)S(1)}, u32[]{:S(2)}, u32[]{:S(2)}) %collective-permute-start.12) | collective-permute-done | bytes 278560 | tf_op jit(solution)/shard_map/ppermute | solution.py:16
  91.3 5.3 %collective-permute-done.13 = bf16[2,136,4,128]{1,2,3,0:T(4,128)(2,1)S(1)} collective-permute-done((bf16[2,136,4,128]{1,2,3,0:T(4,128)(2,1)S(1)}, bf16[2,136,4,128]{1,2,3,0:T(4,128)(2,1)S(1)}, u32[]{:S(2)}, u32[]{:S(2)}) %collective-permute-start.13) | collective-permute-done | bytes 278560 | tf_op jit(solution)/shard_map/ppermute | solution.py:19
  96.8 2.0 collective-permute-start.15
  98.9 2.2 collective-permute-done.14
  101.8 2.6 %pad_maximum_fusion = bf16[2,136,16,136]{1,2,3,0:T(8,128)(2,1)} fusion(bf16[2,136,16,4]{1,2,3,0:T(8,128)(2,1)S(1)} %collective-permute-done.15, bf16[2,136,4,128]{1,2,3,0:T(4,128)(2,1)S(1)} %collective-permute-done.13, bf16[2,136,8,128]{1,2,3,0:T(8,128)(2,1)S(1)} %copy.69, bf16[2,136,4,128]{1,2,3,0:T(4,128)(2,1)S(1)} %collective-permute-done.12, ...), kind=kLoop, calls=%fused_computation.188 | loop fusion | flops 5918720 | bytes 2367488 | tf_op jit(solution)/shard_map/concatenate | solution.py:20
  105.3 14.8 %conditional.14 = (f32[2,32,8,128]{3,2,1,0:T(8,128)S(1)}, f32[2,24,8,128]{3,2,1,0:T(8,128)S(1)}) conditional(s32[]{:T(128)} %convert_element_type.68, (pred[136]{0:T(512)(128)(4,1)S(1)}, bf16[2,136,16,136]{1,2,3,0:T(8,128)(2,1)}, bf16[2,136,16,136]{3,1,2,0:T(8,128)(2,1)S(1)}, bf16[3,3,136,32]{2,3,1,0:T(8,128)(2,1)S(1)}) %tuple.159, () %tuple.79), branch_computations={%region_9.10_spmd, %region_10.11_spmd} | conditional | flops 161024000 | bytes 42584756 | solution.py:142
  105.3 4.6 %copy.72 = bf16[2,136,16,136]{3,1,2,0:T(8,128)(2,1)} copy(bf16[2,136,16,136]{1,2,3,0:T(8,128)(2,1)} %get-tuple-element.198) | data formatting | bytes 2367488 | tf_op jit(solution)/shard_map
  114.0 2.3 copy-done.2
  116.6 3.4 %convolution_bitcast_fusion.4 = f32[2,32,8,128]{3,1,2,0:T(8,128)S(1)} fusion(bf16[2,1224,8,128]{3,1,2,0:T(8,128)(2,1)} %copy-done.2, bf16[1224,32,1,1]{0,1,2,3:T(8,128)(2,1)S(1)} %reshape.60), kind=kOutput, calls=%fused_computation.83 | convolution fusion | flops 160432128 | bytes 5353984 | tf_op jit(solution)/shard_map/cond/branch_0_fun/mkrc,ko->morc/dot_general | solution.py:44
  120.1 4.6 %all_gather.3 = bf16[2,8,8,256]{3,2,1,0:T(8,128)(2,1)S(1)} all-gather(bf16[2,8,8,128]{3,2,1,0:T(8,128)(2,1)S(1)} %slice.832), channel_id=1, replica_groups=mesh['grp'=2,'sp'=4,'sec'=2,'mb'=2] {'sec'}, dimensions={3}, use_global_device_ids=true | all-gather | bytes 98304 | tf_op jit(solution)/shard_map/all_gather | solution.py:172
  125.1 3.5 %collective-permute-start.17 = (bf16[2,16,1,128]{3,2,1,0:T(2,128)(2,1)S(1)}, bf16[2,16,1,128]{3,2,1,0:T(2,128)(2,1)S(1)}, u32[]{:S(2)}, u32[]{:S(2)}) collective-permute-start(bf16[2,16,1,128]{3,2,1,0:T(2,128)(2,1)S(1)} %get-tuple-element.251), channel_id=1, source_target_pairs={{4,0},{8,4},{12,8},{0,12},{5,1},{9,5},{13,9},{1,13},{6,2},{10,6},{... | collective-permute-start | bytes 24584 | tf_op jit(solution)/shard_map/ppermute | solution.py:19
  132.4 4.0 %collective-permute-start.19 = (bf16[2,136,1,128]{3,1,2,0:T(8,128)(2,1)S(1)}, bf16[2,136,1,128]{3,1,2,0:T(8,128)(2,1)S(1)}, u32[]{:S(2)}, u32[]{:S(2)}) collective-permute-start(bf16[2,136,1,128]{3,1,2,0:T(8,128)(2,1)S(1)} %get-tuple-element.239), channel_id=1, source_target_pairs={{4,0},{8,4},{12,8},{0,12},{5,1},{9,5},{13,9},{1,13},{6,2},{10,6},{... | collective-permute-start | bytes 208904 | tf_op jit(solution)/shard_map/ppermute | solution.py:19
  136.4 2.2 collective-permute-done.18
  140.5 15.9 %psum.15 = bf16[2,8,8,128]{3,2,1,0:T(8,128)(2,1)S(1)} all-reduce(bf16[2,8,8,128]{3,2,1,0:T(8,128)(2,1)S(1)} %fusion.77), channel_id=1, replica_groups=mesh['grp'=2,'sp'=4,'sec'=2,'mb'=2] {'sec'}, use_global_device_ids=true, to_apply=%region_15.16 | all-reduce | flops 16384 | bytes 65536 | tf_op jit(solution)/shard_map/psum | solution.py:26
  157.9 2.6 %collective-permute-start.21 = (bf16[2,32,1,128]{3,2,1,0:T(2,128)(2,1)S(1)}, bf16[2,32,1,128]{3,2,1,0:T(2,128)(2,1)S(1)}, u32[]{:S(2)}, u32[]{:S(2)}) collective-permute-start(bf16[2,32,1,128]{3,2,1,0:T(2,128)(2,1)S(1)} %get-tuple-element.247), channel_id=1, source_target_pairs={{4,0},{8,4},{12,8},{0,12},{5,1},{9,5},{13,9},{1,13},{6,2},{10,6},{... | collective-permute-start | bytes 49160 | tf_op jit(solution)/shard_map/ppermute | solution.py:19
  164.8 4.3 %collective-permute-done.22 = bf16[2,32,10,1]{3,2,1,0:T(8,128)(2,1)S(1)} collective-permute-done((bf16[2,32,10,1]{3,2,1,0:T(8,128)(2,1)S(1)}, bf16[2,32,10,1]{3,2,1,0:T(8,128)(2,1)S(1)}, u32[]{:S(2)}, u32[]{:S(2)}) %collective-permute-start.22) | collective-permute-done | bytes 1312 | tf_op jit(solution)/shard_map/ppermute | solution.py:16
  169.1 2.8 %collective-permute-done.23 = bf16[2,32,10,1]{3,2,1,0:T(8,128)(2,1)S(1)} collective-permute-done((bf16[2,32,10,1]{3,2,1,0:T(8,128)(2,1)S(1)}, bf16[2,32,10,1]{3,2,1,0:T(8,128)(2,1)S(1)}, u32[]{:S(2)}, u32[]{:S(2)}) %collective-permute-start.23) | collective-permute-done | bytes 1312 | tf_op jit(solution)/shard_map/ppermute | solution.py:19
  172.5 2.7 %conditional.17 = (bf16[2,136,8,128]{3,1,2,0:T(8,128)(2,1)S(1)}) conditional(s32[]{:T(128)} %convert_element_type.68, (pred[130]{0:T(512)(128)(4,1)}, bf16[2,32,10,130]{3,2,1,0:T(8,128)(2,1)S(1)}, bf16[2,32,10,130]{3,1,2,0:T(8,128)(2,1)S(1)}, bf16[3,3,32,136]{3,2,1,0:T(8,128)(2,1)}) %tuple.84, () %tuple.85), branch_computations={%region_16.17_spmd, %region_17.18_spmd} | conditional | flops 163022080 | bytes 4987046 | solution.py:142
  178.8 2.7 %collective-permute-start.25 = (bf16[2,136,2,128]{1,3,2,0:T(8,128)(2,1)S(1)}, bf16[2,136,2,128]{1,3,2,0:T(8,128)(2,1)S(1)}, u32[]{:S(2)}, u32[]{:S(2)}) collective-permute-start(bf16[2,136,2,128]{1,3,2,0:T(8,128)(2,1)S(1)} %get-tuple-element.233), channel_id=1, source_target_pairs={{4,0},{8,4},{12,8},{0,12},{5,1},{9,5},{13,9},{1,13},{6,2},{10,6},{... | collective-permute-start | bytes 417800 | tf_op jit(solution)/shard_map/ppermute | solution.py:19
  181.5 4.4 %collective-permute-done.24 = bf16[2,136,2,128]{1,3,2,0:T(8,128)(2,1)S(1)} collective-permute-done((bf16[2,136,2,128]{1,3,2,0:T(8,128)(2,1)S(1)}, bf16[2,136,2,128]{1,3,2,0:T(8,128)(2,1)S(1)}, u32[]{:S(2)}, u32[]{:S(2)}) %collective-permute-start.24) | collective-permute-done | bytes 139296 | tf_op jit(solution)/shard_map/ppermute | solution.py:16
  185.9 2.1 collective-permute-done.25
  194.1 9.4 %conditional.18 = (bf16[2,136,8,128]{3,1,2,0:T(8,128)(2,1)S(1)}) conditional(s32[]{:T(128)} %convert_element_type.68, (pred[132]{0:T(512)(128)(4,1)S(1)}, bf16[2,136,12,132]{1,3,2,0:T(8,128)(2,1)}, bf16[2,136,12,132]{3,1,2,0:T(8,128)(2,1)}, bf16[3,3,136,136]{3,2,1,0:T(8,128)(2,1)}) %tuple.164, () %tuple.87), branch_computations={%region_18.19_spmd, %region_19.20_spmd} | conditional | flops 684774144 | bytes 21570856 | solution.py:142
  194.1 3.8 %copy.83 = bf16[2,136,12,132]{3,1,2,0:T(8,128)(2,1)} copy(bf16[2,136,12,132]{1,3,2,0:T(8,128)(2,1)} %get-tuple-element.210) | data formatting | bytes 1723392 | tf_op jit(solution)/shard_map
  197.9 2.1 broadcast_select_fusion.3
  207.7 2.7 %collective-permute-start.29 = (bf16[2,136,4,128]{1,2,3,0:T(4,128)(2,1)S(1)}, bf16[2,136,4,128]{1,2,3,0:T(4,128)(2,1)S(1)}, u32[]{:S(2)}, u32[]{:S(2)}) collective-permute-start(bf16[2,136,4,128]{1,2,3,0:T(4,128)(2,1)S(1)} %get-tuple-element.231), channel_id=1, source_target_pairs={{4,0},{8,4},{12,8},{0,12},{5,1},{9,5},{13,9},{1,13},{6,2},{10,6},{... | collective-permute-start | bytes 835592 | tf_op jit(solution)/shard_map/ppermute | solution.py:19
  210.3 7.3 %collective-permute-done.28 = bf16[2,136,4,128]{1,2,3,0:T(4,128)(2,1)S(1)} collective-permute-done((bf16[2,136,4,128]{1,2,3,0:T(4,128)(2,1)S(1)}, bf16[2,136,4,128]{1,2,3,0:T(4,128)(2,1)S(1)}, u32[]{:S(2)}, u32[]{:S(2)}) %collective-permute-start.28) | collective-permute-done | bytes 278560 | tf_op jit(solution)/shard_map/ppermute | solution.py:16
  217.6 4.9 %collective-permute-done.29 = bf16[2,136,4,128]{1,2,3,0:T(4,128)(2,1)S(1)} collective-permute-done((bf16[2,136,4,128]{1,2,3,0:T(4,128)(2,1)S(1)}, bf16[2,136,4,128]{1,2,3,0:T(4,128)(2,1)S(1)}, u32[]{:S(2)}, u32[]{:S(2)}) %collective-permute-start.29) | collective-permute-done | bytes 278560 | tf_op jit(solution)/shard_map/ppermute | solution.py:19
  222.6 2.0 collective-permute-start.31
  224.6 2.2 collective-permute-done.30
  227.6 2.6 %pad_maximum_fusion.1 = bf16[2,136,16,136]{1,2,3,0:T(8,128)(2,1)} fusion(bf16[2,136,16,4]{1,2,3,0:T(8,128)(2,1)S(1)} %collective-permute-done.31, bf16[2,136,4,128]{1,2,3,0:T(4,128)(2,1)S(1)} %collective-permute-done.29, bf16[2,136,8,128]{1,2,3,0:T(8,128)(2,1)S(1)} %copy.84, bf16[2,136,4,128]{1,2,3,0:T(4,128)(2,1)S(1)} %collective-permute-done.28, ...), kind=kLoop, calls=%fused_computation.189 | loop fusion | flops 5918720 | bytes 2367488 | tf_op jit(solution)/shard_map/concatenate | solution.py:20
  230.2 14.7 %conditional.19 = (f32[2,24,8,128]{3,2,1,0:T(8,128)S(1)}) conditional(s32[]{:T(128)} %convert_element_type.68, (pred[136]{0:T(512)(128)(4,1)S(1)}, bf16[2,136,16,136]{1,2,3,0:T(8,128)(2,1)}, bf16[2,136,16,136]{3,1,2,0:T(8,128)(2,1)S(1)}, bf16[3,3,136,32]{2,3,1,0:T(8,128)(2,1)S(1)}) %tuple.163, () %tuple.89), branch_computations={%region_20.21_spmd, %region_21.22_spmd} | conditional | flops 161024000 | bytes 42453676 | solution.py:142
  230.2 4.6 %copy.87 = bf16[2,136,16,136]{3,1,2,0:T(8,128)(2,1)} copy(bf16[2,136,16,136]{1,2,3,0:T(8,128)(2,1)} %get-tuple-element.214) | data formatting | bytes 2367488 | tf_op jit(solution)/shard_map
  238.9 2.3 copy-done.3
  241.4 3.4 %convolution_bitcast_fusion.9 = f32[2,32,8,128]{3,1,2,0:T(8,128)S(1)} fusion(bf16[2,1224,8,128]{3,1,2,0:T(8,128)(2,1)} %copy-done.3, bf16[1224,32,1,1]{0,1,2,3:T(8,128)(2,1)S(1)} %reshape.65), kind=kOutput, calls=%fused_computation.177 | convolution fusion | flops 160432128 | bytes 5353984 | tf_op jit(solution)/shard_map/cond/branch_0_fun/mkrc,ko->morc/dot_general | solution.py:44
  (208 shorter events, 78.0 us)
Async XLA Ops:
  2.2 6.8 %collective-permute-start = (bf16[2,16,1,128]{3,1,2,0:T(8,128)(2,1)S(1)}, bf16[2,16,1,128]{3,1,2,0:T(8,128)(2,1)S(1)}, u32[]{:S(2)}, u32[]{:S(2)}) collective-permute-start(bf16[2,16,1,128]{3,1,2,0:T(8,128)(2,1)S(1)} %get-tuple-element.252), channel_id=1, source_target_pairs={{0,4},{4,8},{8,12},{12,0},{1,5},{5,9},{9,13},{13,1},{2,6},{6,10},{... | collective-permute-start | bytes 24584 | tf_op jit(solution)/shard_map/ppermute | solution.py:16
  5.3 3.7 %collective-permute-start.1 = (bf16[2,16,1,128]{3,1,2,0:T(8,128)(2,1)S(1)}, bf16[2,16,1,128]{3,1,2,0:T(8,128)(2,1)S(1)}, u32[]{:S(2)}, u32[]{:S(2)}) collective-permute-start(bf16[2,16,1,128]{3,1,2,0:T(8,128)(2,1)S(1)} %get-tuple-element.253), channel_id=1, source_target_pairs={{4,0},{8,4},{12,8},{0,12},{5,1},{9,5},{13,9},{1,13},{6,2},{10,6},{... | collective-permute-start | bytes 24584 | tf_op jit(solution)/shard_map/ppermute | solution.py:19
  9.0 4.1 %copy-start.8 = (bf16[2,24,8,128]{3,2,1,0:T(8,128)(2,1)S(1)}, bf16[2,24,8,128]{3,2,1,0:T(8,128)(2,1)}, u32[]{:S(2)}) copy-start(bf16[2,24,8,128]{3,2,1,0:T(8,128)(2,1)} %param.29) | copy-start | bytes 294916
  9.1 4.1 %copy-start.16 = (s32[8,128]{1,0:T(8,128)S(1)}, s32[8,128]{1,0:T(8,128)}, u32[]{:S(2)}) copy-start(s32[8,128]{1,0:T(8,128)} %param.32) | copy-start | bytes 12292
  9.1 6.8 %copy-start.10 = (bf16[3,3,136,8]{2,3,1,0:T(8,128)(2,1)S(1)}, bf16[3,3,136,8]{2,3,1,0:T(8,128)(2,1)}, u32[]{:S(2)}) copy-start(bf16[3,3,136,8]{2,3,1,0:T(8,128)(2,1)} %param.37) | copy-start | bytes 58756
  9.2 6.4 %collective-permute-start.2 = (bf16[2,136,1,128]{3,1,2,0:T(8,128)(2,1)S(1)}, bf16[2,136,1,128]{3,1,2,0:T(8,128)(2,1)S(1)}, u32[]{:S(2)}, u32[]{:S(2)}) collective-permute-start(bf16[2,136,1,128]{3,1,2,0:T(8,128)(2,1)S(1)} %get-tuple-element.240), channel_id=1, source_target_pairs={{0,4},{4,8},{8,12},{12,0},{1,5},{5,9},{9,13},{13,1},{2,6},{6,10},{... | collective-permute-start | bytes 208904 | tf_op jit(solution)/shard_map/ppermute | solution.py:16
  10.7 5.1 %collective-permute-start.3 = (bf16[2,136,1,128]{3,1,2,0:T(8,128)(2,1)S(1)}, bf16[2,136,1,128]{3,1,2,0:T(8,128)(2,1)S(1)}, u32[]{:S(2)}, u32[]{:S(2)}) collective-permute-start(bf16[2,136,1,128]{3,1,2,0:T(8,128)(2,1)S(1)} %get-tuple-element.241), channel_id=1, source_target_pairs={{4,0},{8,4},{12,8},{0,12},{5,1},{9,5},{13,9},{1,13},{6,2},{10,6},{... | collective-permute-start | bytes 208904 | tf_op jit(solution)/shard_map/ppermute | solution.py:19
  13.2 2.8 %copy-start.14 = (f32[8,128]{1,0:T(8,128)}, f32[8,128]{1,0:T(8,128)S(1)}, u32[]{:S(2)}) copy-start(f32[8,128]{1,0:T(8,128)S(1)} %convert_element_type.70) | copy-start | bytes 12292
  15.9 31.4 %copy-start.23 = (bf16[3,3,32,136]{3,2,1,0:T(8,128)(2,1)S(1)}, bf16[3,3,32,136]{3,2,1,0:T(8,128)(2,1)}, u32[]{:S(2)}) copy-start(bf16[3,3,32,136]{3,2,1,0:T(8,128)(2,1)} %param.33) | copy-start | bytes 235012
  34.2 5.6 %collective-permute-start.4 = (bf16[2,32,1,128]{3,1,2,0:T(8,128)(2,1)S(1)}, bf16[2,32,1,128]{3,1,2,0:T(8,128)(2,1)S(1)}, u32[]{:S(2)}, u32[]{:S(2)}) collective-permute-start(bf16[2,32,1,128]{3,1,2,0:T(8,128)(2,1)S(1)} %get-tuple-element.248), channel_id=1, source_target_pairs={{0,4},{4,8},{8,12},{12,0},{1,5},{5,9},{9,13},{13,1},{2,6},{6,10},{... | collective-permute-start | bytes 49160 | tf_op jit(solution)/shard_map/ppermute | solution.py:16
  35.3 4.5 %collective-permute-start.5 = (bf16[2,32,1,128]{3,1,2,0:T(8,128)(2,1)S(1)}, bf16[2,32,1,128]{3,1,2,0:T(8,128)(2,1)S(1)}, u32[]{:S(2)}, u32[]{:S(2)}) collective-permute-start(bf16[2,32,1,128]{3,1,2,0:T(8,128)(2,1)S(1)} %get-tuple-element.249), channel_id=1, source_target_pairs={{4,0},{8,4},{12,8},{0,12},{5,1},{9,5},{13,9},{1,13},{6,2},{10,6},{... | collective-permute-start | bytes 49160 | tf_op jit(solution)/shard_map/ppermute | solution.py:19
  40.0 5.4 %collective-permute-start.6 = (bf16[2,32,10,1]{3,1,2,0:T(8,128)(2,1)S(1)}, bf16[2,32,10,1]{3,1,2,0:T(8,128)(2,1)S(1)}, u32[]{:S(2)}, u32[]{:S(2)}) collective-permute-start(bf16[2,32,10,1]{3,1,2,0:T(8,128)(2,1)S(1)} %get-tuple-element.244), channel_id=1, source_target_pairs={{0,2},{2,0},{1,3},{3,1},{4,6},{6,4},{5,7},{7,5},{8,10},{10,8},{9,1... | collective-permute-start | bytes 3848 | tf_op jit(solution)/shard_map/ppermute | solution.py:16
  40.1 7.0 %collective-permute-start.7 = (bf16[2,32,10,1]{3,1,2,0:T(8,128)(2,1)S(1)}, bf16[2,32,10,1]{3,1,2,0:T(8,128)(2,1)S(1)}, u32[]{:S(2)}, u32[]{:S(2)}) collective-permute-start(bf16[2,32,10,1]{3,1,2,0:T(8,128)(2,1)S(1)} %get-tuple-element.245), channel_id=1, source_target_pairs={{2,0},{0,2},{3,1},{1,3},{6,4},{4,6},{7,5},{5,7},{10,8},{8,10},{11,... | collective-permute-start | bytes 3848 | tf_op jit(solution)/shard_map/ppermute | solution.py:19
  50.2 8.3 %collective-permute-start.8 = (bf16[2,136,2,128]{1,3,2,0:T(8,128)(2,1)S(1)}, bf16[2,136,2,128]{1,3,2,0:T(8,128)(2,1)S(1)}, u32[]{:S(2)}, u32[]{:S(2)}) collective-permute-start(bf16[2,136,2,128]{1,3,2,0:T(8,128)(2,1)S(1)} %get-tuple-element.236), channel_id=1, source_target_pairs={{0,4},{4,8},{8,12},{12,0},{1,5},{5,9},{9,13},{13,1},{2,6},{6,10},{... | collective-permute-start | bytes 417800 | tf_op jit(solution)/shard_map/ppermute | solution.py:16
  51.4 9.2 %collective-permute-start.9 = (bf16[2,136,2,128]{1,3,2,0:T(8,128)(2,1)S(1)}, bf16[2,136,2,128]{1,3,2,0:T(8,128)(2,1)S(1)}, u32[]{:S(2)}, u32[]{:S(2)}) collective-permute-start(bf16[2,136,2,128]{1,3,2,0:T(8,128)(2,1)S(1)} %get-tuple-element.237), channel_id=1, source_target_pairs={{4,0},{8,4},{12,8},{0,12},{5,1},{9,5},{13,9},{1,13},{6,2},{10,6},{... | collective-permute-start | bytes 417800 | tf_op jit(solution)/shard_map/ppermute | solution.py:19
  60.5 3.9 %copy-start.4 = (bf16[2,136,2,128]{1,3,2,0:T(8,128)(2,1)}, bf16[2,136,2,128]{1,3,2,0:T(8,128)(2,1)S(1)}, u32[]{:S(2)}) copy-start(bf16[2,136,2,128]{1,3,2,0:T(8,128)(2,1)S(1)} %collective-permute-done.9) | copy-start | bytes 417796
  60.6 3.9 %collective-permute-start.10 = (bf16[2,136,12,2]{1,3,2,0:T(2,128)(2,1)S(1)}, bf16[2,136,12,2]{1,3,2,0:T(2,128)(2,1)S(1)}, u32[]{:S(2)}, u32[]{:S(2)}) collective-permute-start(bf16[2,136,12,2]{1,3,2,0:T(2,128)(2,1)S(1)} %get-tuple-element.228), channel_id=1, source_target_pairs={{0,2},{2,0},{1,3},{3,1},{4,6},{6,4},{5,7},{7,5},{8,10},{10,8},{9,1... | collective-permute-start | bytes 39176 | tf_op jit(solution)/shard_map/ppermute | solution.py:16
  60.7 4.1 %collective-permute-start.11 = (bf16[2,136,12,2]{1,3,2,0:T(2,128)(2,1)S(1)}, bf16[2,136,12,2]{1,3,2,0:T(2,128)(2,1)S(1)}, u32[]{:S(2)}, u32[]{:S(2)}) collective-permute-start(bf16[2,136,12,2]{1,3,2,0:T(2,128)(2,1)S(1)} %get-tuple-element.229), channel_id=1, source_target_pairs={{2,0},{0,2},{3,1},{1,3},{6,4},{4,6},{7,5},{5,7},{10,8},{8,10},{11,... | collective-permute-start | bytes 39176 | tf_op jit(solution)/shard_map/ppermute | solution.py:19
  62.7 5.1 %copy-start.19 = (pred[132]{0:T(512)(128)(4,1)}, pred[132]{0:T(512)(128)(4,1)S(1)}, u32[]{:S(2)}) copy-start(pred[132]{0:T(512)(128)(4,1)S(1)} %compare_and_fusion.1) | copy-start | bytes 400
  77.9 13.4 %collective-permute-start.12 = (bf16[2,136,4,128]{1,2,3,0:T(4,128)(2,1)}, bf16[2,136,4,128]{1,2,3,0:T(4,128)(2,1)S(1)}, u32[]{:S(2)}, u32[]{:S(2)}) collective-permute-start(bf16[2,136,4,128]{1,2,3,0:T(4,128)(2,1)} %get-tuple-element.234), channel_id=1, source_target_pairs={{0,4},{4,8},{8,12},{12,0},{1,5},{5,9},{9,13},{13,1},{2,6},{6,10},{... | collective-permute-start | bytes 835592 | tf_op jit(solution)/shard_map/ppermute | solution.py:16
  79.2 17.4 %collective-permute-start.13 = (bf16[2,136,4,128]{1,2,3,0:T(4,128)(2,1)S(1)}, bf16[2,136,4,128]{1,2,3,0:T(4,128)(2,1)S(1)}, u32[]{:S(2)}, u32[]{:S(2)}) collective-permute-start(bf16[2,136,4,128]{1,2,3,0:T(4,128)(2,1)S(1)} %get-tuple-element.235), channel_id=1, source_target_pairs={{4,0},{8,4},{12,8},{0,12},{5,1},{9,5},{13,9},{1,13},{6,2},{10,6},{... | collective-permute-start | bytes 835592 | tf_op jit(solution)/shard_map/ppermute | solution.py:19
  96.8 4.3 %collective-permute-start.14 = (bf16[2,136,16,4]{1,2,3,0:T(8,128)(2,1)S(1)}, bf16[2,136,16,4]{1,2,3,0:T(8,128)(2,1)S(1)}, u32[]{:S(2)}, u32[]{:S(2)}) collective-permute-start(bf16[2,136,16,4]{1,2,3,0:T(8,128)(2,1)S(1)} %get-tuple-element.224), channel_id=1, source_target_pairs={{0,2},{2,0},{1,3},{3,1},{4,6},{6,4},{5,7},{7,5},{8,10},{10,8},{9,1... | collective-permute-start | bytes 104456 | tf_op jit(solution)/shard_map/ppermute | solution.py:16
  96.8 5.0 %collective-permute-start.15 = (bf16[2,136,16,4]{1,2,3,0:T(8,128)(2,1)S(1)}, bf16[2,136,16,4]{1,2,3,0:T(8,128)(2,1)S(1)}, u32[]{:S(2)}, u32[]{:S(2)}) collective-permute-start(bf16[2,136,16,4]{1,2,3,0:T(8,128)(2,1)S(1)} %get-tuple-element.225), channel_id=1, source_target_pairs={{2,0},{0,2},{3,1},{1,3},{6,4},{4,6},{7,5},{5,7},{10,8},{8,10},{11,... | collective-permute-start | bytes 104456 | tf_op jit(solution)/shard_map/ppermute | solution.py:19
  98.9 6.5 %copy-start.17 = (pred[136]{0:T(512)(128)(4,1)}, pred[136]{0:T(512)(128)(4,1)S(1)}, u32[]{:S(2)}) copy-start(pred[136]{0:T(512)(128)(4,1)S(1)} %compare_and_fusion.2) | copy-start | bytes 412
  114.0 2.3 copy-start.2
  124.8 5.6 %collective-permute-start.16 = (bf16[2,16,1,128]{3,2,1,0:T(2,128)(2,1)S(1)}, bf16[2,16,1,128]{3,2,1,0:T(2,128)(2,1)S(1)}, u32[]{:S(2)}, u32[]{:S(2)}) collective-permute-start(bf16[2,16,1,128]{3,2,1,0:T(2,128)(2,1)S(1)} %get-tuple-element.250), channel_id=1, source_target_pairs={{0,4},{4,8},{8,12},{12,0},{1,5},{5,9},{9,13},{13,1},{2,6},{6,10},{... | collective-permute-start | bytes 24584 | tf_op jit(solution)/shard_map/ppermute | solution.py:16
  125.1 5.2 %collective-permute-start.17 = (bf16[2,16,1,128]{3,2,1,0:T(2,128)(2,1)S(1)}, bf16[2,16,1,128]{3,2,1,0:T(2,128)(2,1)S(1)}, u32[]{:S(2)}, u32[]{:S(2)}) collective-permute-start(bf16[2,16,1,128]{3,2,1,0:T(2,128)(2,1)S(1)} %get-tuple-element.251), channel_id=1, source_target_pairs={{4,0},{8,4},{12,8},{0,12},{5,1},{9,5},{13,9},{1,13},{6,2},{10,6},{... | collective-permute-start | bytes 24584 | tf_op jit(solution)/shard_map/ppermute | solution.py:19
  130.5 6.0 %copy-start.9 = (bf16[2,24,8,128]{3,2,1,0:T(8,128)(2,1)S(1)}, bf16[2,24,8,128]{3,2,1,0:T(8,128)(2,1)}, u32[]{:S(2)}) copy-start(bf16[2,24,8,128]{3,2,1,0:T(8,128)(2,1)} %param.29) | copy-start | bytes 294916
  130.5 9.3 %copy-start.11 = (bf16[3,3,136,8]{2,3,1,0:T(8,128)(2,1)S(1)}, bf16[3,3,136,8]{2,3,1,0:T(8,128)(2,1)}, u32[]{:S(2)}) copy-start(bf16[3,3,136,8]{2,3,1,0:T(8,128)(2,1)} %param.37) | copy-start | bytes 58756
  132.3 6.3 %collective-permute-start.18 = (bf16[2,136,1,128]{3,1,2,0:T(8,128)(2,1)S(1)}, bf16[2,136,1,128]{3,1,2,0:T(8,128)(2,1)S(1)}, u32[]{:S(2)}, u32[]{:S(2)}) collective-permute-start(bf16[2,136,1,128]{3,1,2,0:T(8,128)(2,1)S(1)} %get-tuple-element.238), channel_id=1, source_target_pairs={{0,4},{4,8},{8,12},{12,0},{1,5},{5,9},{9,13},{13,1},{2,6},{6,10},{... | collective-permute-start | bytes 208904 | tf_op jit(solution)/shard_map/ppermute | solution.py:16
  132.4 6.3 %collective-permute-start.19 = (bf16[2,136,1,128]{3,1,2,0:T(8,128)(2,1)S(1)}, bf16[2,136,1,128]{3,1,2,0:T(8,128)(2,1)S(1)}, u32[]{:S(2)}, u32[]{:S(2)}) collective-permute-start(bf16[2,136,1,128]{3,1,2,0:T(8,128)(2,1)S(1)} %get-tuple-element.239), channel_id=1, source_target_pairs={{4,0},{8,4},{12,8},{0,12},{5,1},{9,5},{13,9},{1,13},{6,2},{10,6},{... | collective-permute-start | bytes 208904 | tf_op jit(solution)/shard_map/ppermute | solution.py:19
  156.5 16.1 %copy-start.12 = (bf16[2,8,8,128]{3,2,1,0:T(8,128)(2,1)}, bf16[2,8,8,128]{3,2,1,0:T(8,128)(2,1)S(1)}, u32[]{:S(2)}) copy-start(bf16[2,8,8,128]{3,2,1,0:T(8,128)(2,1)S(1)} %psum.15) | copy-start | bytes 98308
  156.6 5.8 %collective-permute-start.20 = (bf16[2,32,1,128]{3,2,1,0:T(2,128)(2,1)S(1)}, bf16[2,32,1,128]{3,2,1,0:T(2,128)(2,1)S(1)}, u32[]{:S(2)}, u32[]{:S(2)}) collective-permute-start(bf16[2,32,1,128]{3,2,1,0:T(2,128)(2,1)S(1)} %get-tuple-element.246), channel_id=1, source_target_pairs={{0,4},{4,8},{8,12},{12,0},{1,5},{5,9},{9,13},{13,1},{2,6},{6,10},{... | collective-permute-start | bytes 49160 | tf_op jit(solution)/shard_map/ppermute | solution.py:16
  157.9 4.5 %collective-permute-start.21 = (bf16[2,32,1,128]{3,2,1,0:T(2,128)(2,1)S(1)}, bf16[2,32,1,128]{3,2,1,0:T(2,128)(2,1)S(1)}, u32[]{:S(2)}, u32[]{:S(2)}) collective-permute-start(bf16[2,32,1,128]{3,2,1,0:T(2,128)(2,1)S(1)} %get-tuple-element.247), channel_id=1, source_target_pairs={{4,0},{8,4},{12,8},{0,12},{5,1},{9,5},{13,9},{1,13},{6,2},{10,6},{... | collective-permute-start | bytes 49160 | tf_op jit(solution)/shard_map/ppermute | solution.py:19
  162.7 6.4 %collective-permute-start.22 = (bf16[2,32,10,1]{3,2,1,0:T(8,128)(2,1)S(1)}, bf16[2,32,10,1]{3,2,1,0:T(8,128)(2,1)S(1)}, u32[]{:S(2)}, u32[]{:S(2)}) collective-permute-start(bf16[2,32,10,1]{3,2,1,0:T(8,128)(2,1)S(1)} %get-tuple-element.242), channel_id=1, source_target_pairs={{0,2},{2,0},{1,3},{3,1},{4,6},{6,4},{5,7},{7,5},{8,10},{10,8},{9,1... | collective-permute-start | bytes 3848 | tf_op jit(solution)/shard_map/ppermute | solution.py:16
  162.8 9.1 %collective-permute-start.23 = (bf16[2,32,10,1]{3,2,1,0:T(8,128)(2,1)S(1)}, bf16[2,32,10,1]{3,2,1,0:T(8,128)(2,1)S(1)}, u32[]{:S(2)}, u32[]{:S(2)}) collective-permute-start(bf16[2,32,10,1]{3,2,1,0:T(8,128)(2,1)S(1)} %get-tuple-element.243), channel_id=1, source_target_pairs={{2,0},{0,2},{3,1},{1,3},{6,4},{4,6},{7,5},{5,7},{10,8},{8,10},{11,... | collective-permute-start | bytes 3848 | tf_op jit(solution)/shard_map/ppermute | solution.py:19
  172.8 1.7 copy-start.24
  177.5 8.4 %collective-permute-start.24 = (bf16[2,136,2,128]{1,3,2,0:T(8,128)(2,1)S(1)}, bf16[2,136,2,128]{1,3,2,0:T(8,128)(2,1)S(1)}, u32[]{:S(2)}, u32[]{:S(2)}) collective-permute-start(bf16[2,136,2,128]{1,3,2,0:T(8,128)(2,1)S(1)} %get-tuple-element.232), channel_id=1, source_target_pairs={{0,4},{4,8},{8,12},{12,0},{1,5},{5,9},{9,13},{13,1},{2,6},{6,10},{... | collective-permute-start | bytes 417800 | tf_op jit(solution)/shard_map/ppermute | solution.py:16
  178.8 15.3 %copy-start.20 = (pred[132]{0:T(512)(128)(4,1)S(1)}, pred[132]{0:T(512)(128)(4,1)}, u32[]{:S(2)}) copy-start(pred[132]{0:T(512)(128)(4,1)} %copy-done.19) | copy-start | bytes 400
  178.8 9.2 %collective-permute-start.25 = (bf16[2,136,2,128]{1,3,2,0:T(8,128)(2,1)S(1)}, bf16[2,136,2,128]{1,3,2,0:T(8,128)(2,1)S(1)}, u32[]{:S(2)}, u32[]{:S(2)}) collective-permute-start(bf16[2,136,2,128]{1,3,2,0:T(8,128)(2,1)S(1)} %get-tuple-element.233), channel_id=1, source_target_pairs={{4,0},{8,4},{12,8},{0,12},{5,1},{9,5},{13,9},{1,13},{6,2},{10,6},{... | collective-permute-start | bytes 417800 | tf_op jit(solution)/shard_map/ppermute | solution.py:19
  188.1 3.9 %collective-permute-start.26 = (bf16[2,136,12,2]{1,3,2,0:T(2,128)(2,1)S(1)}, bf16[2,136,12,2]{1,3,2,0:T(2,128)(2,1)S(1)}, u32[]{:S(2)}, u32[]{:S(2)}) collective-permute-start(bf16[2,136,12,2]{1,3,2,0:T(2,128)(2,1)S(1)} %get-tuple-element.226), channel_id=1, source_target_pairs={{0,2},{2,0},{1,3},{3,1},{4,6},{6,4},{5,7},{7,5},{8,10},{10,8},{9,1... | collective-permute-start | bytes 39176 | tf_op jit(solution)/shard_map/ppermute | solution.py:16
  188.1 4.1 %collective-permute-start.27 = (bf16[2,136,12,2]{1,3,2,0:T(2,128)(2,1)S(1)}, bf16[2,136,12,2]{1,3,2,0:T(2,128)(2,1)S(1)}, u32[]{:S(2)}, u32[]{:S(2)}) collective-permute-start(bf16[2,136,12,2]{1,3,2,0:T(2,128)(2,1)S(1)} %get-tuple-element.227), channel_id=1, source_target_pairs={{2,0},{0,2},{3,1},{1,3},{6,4},{4,6},{7,5},{5,7},{10,8},{8,10},{11,... | collective-permute-start | bytes 39176 | tf_op jit(solution)/shard_map/ppermute | solution.py:19
  206.5 11.1 %collective-permute-start.28 = (bf16[2,136,4,128]{1,2,3,0:T(4,128)(2,1)S(1)}, bf16[2,136,4,128]{1,2,3,0:T(4,128)(2,1)S(1)}, u32[]{:S(2)}, u32[]{:S(2)}) collective-permute-start(bf16[2,136,4,128]{1,2,3,0:T(4,128)(2,1)S(1)} %get-tuple-element.230), channel_id=1, source_target_pairs={{0,4},{4,8},{8,12},{12,0},{1,5},{5,9},{9,13},{13,1},{2,6},{6,10},{... | collective-permute-start | bytes 835592 | tf_op jit(solution)/shard_map/ppermute | solution.py:16
  207.7 14.8 %collective-permute-start.29 = (bf16[2,136,4,128]{1,2,3,0:T(4,128)(2,1)S(1)}, bf16[2,136,4,128]{1,2,3,0:T(4,128)(2,1)S(1)}, u32[]{:S(2)}, u32[]{:S(2)}) collective-permute-start(bf16[2,136,4,128]{1,2,3,0:T(4,128)(2,1)S(1)} %get-tuple-element.231), channel_id=1, source_target_pairs={{4,0},{8,4},{12,8},{0,12},{5,1},{9,5},{13,9},{1,13},{6,2},{10,6},{... | collective-permute-start | bytes 835592 | tf_op jit(solution)/shard_map/ppermute | solution.py:19
  222.5 4.3 %collective-permute-start.30 = (bf16[2,136,16,4]{1,2,3,0:T(8,128)(2,1)S(1)}, bf16[2,136,16,4]{1,2,3,0:T(8,128)(2,1)S(1)}, u32[]{:S(2)}, u32[]{:S(2)}) collective-permute-start(bf16[2,136,16,4]{1,2,3,0:T(8,128)(2,1)S(1)} %get-tuple-element.222), channel_id=1, source_target_pairs={{0,2},{2,0},{1,3},{3,1},{4,6},{6,4},{5,7},{7,5},{8,10},{10,8},{9,1... | collective-permute-start | bytes 104456 | tf_op jit(solution)/shard_map/ppermute | solution.py:16
  222.6 5.0 %collective-permute-start.31 = (bf16[2,136,16,4]{1,2,3,0:T(8,128)(2,1)S(1)}, bf16[2,136,16,4]{1,2,3,0:T(8,128)(2,1)S(1)}, u32[]{:S(2)}, u32[]{:S(2)}) collective-permute-start(bf16[2,136,16,4]{1,2,3,0:T(8,128)(2,1)S(1)} %get-tuple-element.223), channel_id=1, source_target_pairs={{2,0},{0,2},{3,1},{1,3},{6,4},{4,6},{7,5},{5,7},{10,8},{8,10},{11,... | collective-permute-start | bytes 104456 | tf_op jit(solution)/shard_map/ppermute | solution.py:19
  224.6 5.6 %copy-start.18 = (pred[136]{0:T(512)(128)(4,1)S(1)}, pred[136]{0:T(512)(128)(4,1)}, u32[]{:S(2)}) copy-start(pred[136]{0:T(512)(128)(4,1)} %copy-done.17) | copy-start | bytes 412
  238.8 2.3 copy-start.3
  (7 other events, 6.2 us)
where the time goes:
time: 247 us; the launch traced here: 246 us
  waiting for transfers between devices  73.3 us (30%)
  starting transfers between devices  53.1 us (21%)
  local copies, waits for them, and re-layouts  46.3 us (19%)
  blocking collectives  38 us (15%)
  other arithmetic  22.2 us (9%)
  matrix products  10.6 us (4%)
    ppermute x16, waiting for transfers between devices, with_halo(): lax.ppermute(lax.slice_in_dim(block, block.shape[dim] - width, None, axis...  52.3 us
    ppermute x16, starting transfers between devices, with_halo(): lax.ppermute(lax.slice_in_dim(block, 0, width, axis=dim), axis, backward)  40.1 us
    psum x2, blocking collectives, spread_2(): return lax.psum(kept, axis)  33.4 us
    ppermute x16, waiting for transfers between devices, with_halo(): lax.ppermute(lax.slice_in_dim(block, 0, width, axis=dim), axis, backward)  20.9 us
    another operation x13, local copies, waits for them, and re-layouts  18.2 us
    cond x58, local copies, waits for them, and re-layouts  13.4 us
    ppermute x16, starting transfers between devices, with_halo(): lax.ppermute(lax.slice_in_dim(block, block.shape[dim] - width, None, axis...  13 us
    concatenate x12, other arithmetic, with_halo(): block = jnp.concatenate([low, block, high], axis=dim)  11.2 us
  transfers between devices with their start and end apart: 32, of which 27 were waited for; matrix products, arithmetic and copies ran while one was open for 0% of the time, Pallas kernels for 0%

commit v1 on v0

--- a/solution.py
+++ b/solution.py
@@ -5,6 +5,12 @@
 
 STEPS = 2
 dilations = (1, 2, 4)
+
+
+def add_all(x, mesh_axis):
+    blocks = lax.all_gather(x, mesh_axis, axis=0, tiled=False)
+    result = blocks.sum(axis=0)
+    return result
 
 
 def with_halo(block, sides, width):
@@ -23,7 +29,7 @@
 
 def spread_2(value, axis, source):
     kept = jnp.where(lax.axis_index(axis) == source, value, 0).astype(value.dtype)
-    return lax.psum(kept, axis)
+    return add_all(kept, axis)
 
 
 def tap_sum(source, weight, dilation):

time: 247 us -> 239 us (0.968)
  blocking collectives: 38 us -> 29.6 us
    psum x2 -> x0, blocking collectives: 33.4 us -> none  [spread_2(): return lax.psum(kept, axis)]
    all_gather x0 -> x2, blocking collectives: none -> 25 us  [add_all(): blocks = lax.all_gather(x, mesh_axis, axis=0, tiled=False)]
    ppermute x16, starting transfers between devices: 13 us -> 17.3 us  [with_halo(): lax.ppermute(lax.slice_in_dim(block, block.shape[dim] - width, None, axis...]
    ppermute x16, starting transfers between devices: 40.1 us -> 36.1 us  [with_halo(): lax.ppermute(lax.slice_in_dim(block, 0, width, axis=dim), axis, backward)]
where the time goes in v1:
time: 239 us; the launch traced here: 238 us
  waiting for transfers between devices  73.8 us (31%)
  starting transfers between devices  53.4 us (22%)
  local copies, waits for them, and re-layouts  46.3 us (19%)
  blocking collectives  29.6 us (12%)
  other arithmetic  22.2 us (9%)
  matrix products  10.6 us (4%)
    ppermute x16, waiting for transfers between devices, with_halo(): lax.ppermute(lax.slice_in_dim(block, block.shape[dim] - width, None, axis...  52.6 us
    ppermute x16, starting transfers between devices, with_halo(): lax.ppermute(lax.slice_in_dim(block, 0, width, axis=dim), axis, backward)  36.1 us
    all_gather x2, blocking collectives, add_all(): blocks = lax.all_gather(x, mesh_axis, axis=0, tiled=False)  25 us
    ppermute x16, waiting for transfers between devices, with_halo(): lax.ppermute(lax.slice_in_dim(block, 0, width, axis=dim), axis, backward)  21.2 us
    another operation x13, local copies, waits for them, and re-layouts  18.2 us
    ppermute x16, starting transfers between devices, with_halo(): lax.ppermute(lax.slice_in_dim(block, block.shape[dim] - width, None, axis...  17.3 us
    cond x58, local copies, waits for them, and re-layouts  13.4 us
    concatenate x12, other arithmetic, with_halo(): block = jnp.concatenate([low, block, high], axis=dim)  11.2 us
  transfers between devices with their start and end apart: 32, of which 27 were waited for; matrix products, arithmetic and copies ran while one was open for 0% of the time, Pallas kernels for 0%

profile of v1, /device:TPU:0, one launch (start us, length us, event | category | flops | bytes accessed | tf_op | source)
XLA Modules:
  0.0 238.0 jit_solution(12883848074267271107)
XLA Ops:
  2.2 3.1 %collective-permute-start = (bf16[2,16,1,128]{3,1,2,0:T(8,128)(2,1)S(1)}, bf16[2,16,1,128]{3,1,2,0:T(8,128)(2,1)S(1)}, u32[]{:S(2)}, u32[]{:S(2)}) collective-permute-start(bf16[2,16,1,128]{3,1,2,0:T(8,128)(2,1)S(1)} %get-tuple-element.252), channel_id=1, source_target_pairs={{0,4},{4,8},{8,12},{12,0},{1,5},{5,9},{9,13},{13,1},{2,6},{6,10},{... | collective-permute-start | bytes 24584 | tf_op jit(solution)/shard_map/ppermute | solution.py:22
  5.3 2.1 collective-permute-start.1
  10.7 2.4 collective-permute-start.3
  13.2 2.5 %collective-permute-done.2 = bf16[2,136,1,128]{3,1,2,0:T(8,128)(2,1)S(1)} collective-permute-done((bf16[2,136,1,128]{3,1,2,0:T(8,128)(2,1)S(1)}, bf16[2,136,1,128]{3,1,2,0:T(8,128)(2,1)S(1)}, u32[]{:S(2)}, u32[]{:S(2)}) %collective-permute-start.2) | collective-permute-done | bytes 69664 | tf_op jit(solution)/shard_map/ppermute | solution.py:22
  16.7 13.2 %all-gather = bf16[4,8,8,128]{3,2,1,0:T(8,128)(2,1)S(1)} all-gather(bf16[2,8,8,128]{3,2,1,0:T(8,128)(2,1)S(1)} %fusion.76), channel_id=2, replica_groups=mesh['grp'=2,'sp'=4,'sec'=2,'mb'=2] {'sec'}, dimensions={0}, use_global_device_ids=true | all-gather | bytes 98304 | tf_op jit(solution)/shard_map/all_gather | solution.py:11
  31.0 2.8 %collective-permute-start.5 = (bf16[2,32,1,128]{3,1,2,0:T(8,128)(2,1)S(1)}, bf16[2,32,1,128]{3,1,2,0:T(8,128)(2,1)S(1)}, u32[]{:S(2)}, u32[]{:S(2)}) collective-permute-start(bf16[2,32,1,128]{3,1,2,0:T(8,128)(2,1)S(1)} %get-tuple-element.249), channel_id=1, source_target_pairs={{4,0},{8,4},{12,8},{0,12},{5,1},{9,5},{13,9},{1,13},{6,2},{10,6},{... | collective-permute-start | bytes 49160 | tf_op jit(solution)/shard_map/ppermute | solution.py:25
  35.7 2.1 collective-permute-start.6
  38.4 2.7 %collective-permute-done.6 = bf16[2,32,10,1]{3,1,2,0:T(8,128)(2,1)S(1)} collective-permute-done((bf16[2,32,10,1]{3,1,2,0:T(8,128)(2,1)S(1)}, bf16[2,32,10,1]{3,1,2,0:T(8,128)(2,1)S(1)}, u32[]{:S(2)}, u32[]{:S(2)}) %collective-permute-start.6) | collective-permute-done | bytes 1312 | tf_op jit(solution)/shard_map/ppermute | solution.py:22
  43.3 2.3 conditional.12
  47.3 2.8 %collective-permute-start.9 = (bf16[2,136,2,128]{1,3,2,0:T(8,128)(2,1)S(1)}, bf16[2,136,2,128]{1,3,2,0:T(8,128)(2,1)S(1)}, u32[]{:S(2)}, u32[]{:S(2)}) collective-permute-start(bf16[2,136,2,128]{1,3,2,0:T(8,128)(2,1)S(1)} %get-tuple-element.237), channel_id=1, source_target_pairs={{4,0},{8,4},{12,8},{0,12},{5,1},{9,5},{13,9},{1,13},{6,2},{10,6},{... | collective-permute-start | bytes 417800 | tf_op jit(solution)/shard_map/ppermute | solution.py:25
  50.2 4.4 %collective-permute-done.8 = bf16[2,136,2,128]{1,3,2,0:T(8,128)(2,1)S(1)} collective-permute-done((bf16[2,136,2,128]{1,3,2,0:T(8,128)(2,1)S(1)}, bf16[2,136,2,128]{1,3,2,0:T(8,128)(2,1)S(1)}, u32[]{:S(2)}, u32[]{:S(2)}) %collective-permute-start.8) | collective-permute-done | bytes 139296 | tf_op jit(solution)/shard_map/ppermute | solution.py:22
  63.8 8.1 %conditional.13 = (bf16[2,136,8,128]{3,1,2,0:T(8,128)(2,1)S(1)}) conditional(s32[]{:T(128)} %convert_element_type.72, (pred[132]{0:T(512)(128)(4,1)S(1)}, bf16[2,136,12,132]{1,3,2,0:T(8,128)(2,1)S(1)}, bf16[2,136,12,132]{3,1,2,0:T(8,128)(2,1)}, bf16[3,3,136,136]{3,2,1,0:T(8,128)(2,1)}) %tuple.76, () %tuple.77), branch_computations={%region_7.8_spmd, %region_8.9_spmd} | conditional | flops 684774144 | bytes 21570856 | solution.py:148
  63.8 2.4 %copy.68 = bf16[2,136,12,132]{3,1,2,0:T(8,128)(2,1)} copy(bf16[2,136,12,132]{1,3,2,0:T(8,128)(2,1)S(1)} %get-tuple-element.194) | data formatting | bytes 1723392 | tf_op jit(solution)/shard_map
  66.2 2.1 broadcast_select_fusion.1
  75.2 2.5 %collective-permute-start.13 = (bf16[2,136,4,128]{1,2,3,0:T(4,128)(2,1)S(1)}, bf16[2,136,4,128]{1,2,3,0:T(4,128)(2,1)S(1)}, u32[]{:S(2)}, u32[]{:S(2)}) collective-permute-start(bf16[2,136,4,128]{1,2,3,0:T(4,128)(2,1)S(1)} %get-tuple-element.235), channel_id=1, source_target_pairs={{4,0},{8,4},{12,8},{0,12},{5,1},{9,5},{13,9},{1,13},{6,2},{10,6},{... | collective-permute-start | bytes 835592 | tf_op jit(solution)/shard_map/ppermute | solution.py:25
  77.7 10.0 %collective-permute-done.12 = bf16[2,136,4,128]{1,2,3,0:T(4,128)(2,1)S(1)} collective-permute-done((bf16[2,136,4,128]{1,2,3,0:T(4,128)(2,1)}, bf16[2,136,4,128]{1,2,3,0:T(4,128)(2,1)S(1)}, u32[]{:S(2)}, u32[]{:S(2)}) %collective-permute-start.12) | collective-permute-done | bytes 278560 | tf_op jit(solution)/shard_map/ppermute | solution.py:22
  87.8 5.3 %collective-permute-done.13 = bf16[2,136,4,128]{1,2,3,0:T(4,128)(2,1)S(1)} collective-permute-done((bf16[2,136,4,128]{1,2,3,0:T(4,128)(2,1)S(1)}, bf16[2,136,4,128]{1,2,3,0:T(4,128)(2,1)S(1)}, u32[]{:S(2)}, u32[]{:S(2)}) %collective-permute-start.13) | collective-permute-done | bytes 278560 | tf_op jit(solution)/shard_map/ppermute | solution.py:25
  95.3 2.2 collective-permute-done.14
  98.2 2.6 %pad_maximum_fusion = bf16[2,136,16,136]{1,2,3,0:T(8,128)(2,1)} fusion(bf16[2,136,16,4]{1,2,3,0:T(8,128)(2,1)S(1)} %collective-permute-done.15, bf16[2,136,4,128]{1,2,3,0:T(4,128)(2,1)S(1)} %collective-permute-done.13, bf16[2,136,8,128]{1,2,3,0:T(8,128)(2,1)S(1)} %copy.69, bf16[2,136,4,128]{1,2,3,0:T(4,128)(2,1)S(1)} %collective-permute-done.12, ...), kind=kLoop, calls=%fused_computation.188 | loop fusion | flops 5918720 | bytes 2367488 | tf_op jit(solution)/shard_map/concatenate | solution.py:26
  101.8 14.8 %conditional.14 = (f32[2,32,8,128]{3,2,1,0:T(8,128)S(1)}, f32[2,24,8,128]{3,2,1,0:T(8,128)S(1)}) conditional(s32[]{:T(128)} %convert_element_type.72, (pred[136]{0:T(512)(128)(4,1)S(1)}, bf16[2,136,16,136]{1,2,3,0:T(8,128)(2,1)}, bf16[2,136,16,136]{3,1,2,0:T(8,128)(2,1)S(1)}, bf16[3,3,136,32]{2,3,1,0:T(8,128)(2,1)S(1)}) %tuple.159, () %tuple.79), branch_computations={%region_9.10_spmd, %region_10.11_spmd} | conditional | flops 161024000 | bytes 42584756 | solution.py:148
  101.8 4.6 %copy.72 = bf16[2,136,16,136]{3,1,2,0:T(8,128)(2,1)} copy(bf16[2,136,16,136]{1,2,3,0:T(8,128)(2,1)} %get-tuple-element.198) | data formatting | bytes 2367488 | tf_op jit(solution)/shard_map
  110.4 2.3 copy-done.2
  113.0 3.3 %convolution_bitcast_fusion.4 = f32[2,32,8,128]{3,1,2,0:T(8,128)S(1)} fusion(bf16[2,1224,8,128]{3,1,2,0:T(8,128)(2,1)} %copy-done.2, bf16[1224,32,1,1]{0,1,2,3:T(8,128)(2,1)S(1)} %reshape.62), kind=kOutput, calls=%fused_computation.83 | convolution fusion | flops 160432128 | bytes 5353984 | tf_op jit(solution)/shard_map/cond/branch_0_fun/mkrc,ko->morc/dot_general | solution.py:50
  116.6 4.6 %all_gather.17 = bf16[2,8,8,256]{3,2,1,0:T(8,128)(2,1)S(1)} all-gather(bf16[2,8,8,128]{3,2,1,0:T(8,128)(2,1)S(1)} %slice.832), channel_id=1, replica_groups=mesh['grp'=2,'sp'=4,'sec'=2,'mb'=2] {'sec'}, dimensions={3}, use_global_device_ids=true | all-gather | bytes 98304 | tf_op jit(solution)/shard_map/all_gather | solution.py:178
  121.6 3.5 %collective-permute-start.17 = (bf16[2,16,1,128]{3,2,1,0:T(2,128)(2,1)S(1)}, bf16[2,16,1,128]{3,2,1,0:T(2,128)(2,1)S(1)}, u32[]{:S(2)}, u32[]{:S(2)}) collective-permute-start(bf16[2,16,1,128]{3,2,1,0:T(2,128)(2,1)S(1)} %get-tuple-element.251), channel_id=1, source_target_pairs={{4,0},{8,4},{12,8},{0,12},{5,1},{9,5},{13,9},{1,13},{6,2},{10,6},{... | collective-permute-start | bytes 24584 | tf_op jit(solution)/shard_map/ppermute | solution.py:25
  128.8 3.9 %collective-permute-start.19 = (bf16[2,136,1,128]{3,1,2,0:T(8,128)(2,1)S(1)}, bf16[2,136,1,128]{3,1,2,0:T(8,128)(2,1)S(1)}, u32[]{:S(2)}, u32[]{:S(2)}) collective-permute-start(bf16[2,136,1,128]{3,1,2,0:T(8,128)(2,1)S(1)} %get-tuple-element.239), channel_id=1, source_target_pairs={{4,0},{8,4},{12,8},{0,12},{5,1},{9,5},{13,9},{1,13},{6,2},{10,6},{... | collective-permute-start | bytes 208904 | tf_op jit(solution)/shard_map/ppermute | solution.py:25
  132.7 2.2 collective-permute-done.18
  136.8 11.8 %all-gather.1 = bf16[4,8,8,128]{3,2,1,0:T(8,128)(2,1)S(1)} all-gather(bf16[2,8,8,128]{3,2,1,0:T(8,128)(2,1)S(1)} %fusion.77), channel_id=3, replica_groups=mesh['grp'=2,'sp'=4,'sec'=2,'mb'=2] {'sec'}, dimensions={0}, use_global_device_ids=true | all-gather | bytes 98304 | tf_op jit(solution)/shard_map/all_gather | solution.py:11
  150.4 2.6 %collective-permute-start.21 = (bf16[2,32,1,128]{3,2,1,0:T(2,128)(2,1)S(1)}, bf16[2,32,1,128]{3,2,1,0:T(2,128)(2,1)S(1)}, u32[]{:S(2)}, u32[]{:S(2)}) collective-permute-start(bf16[2,32,1,128]{3,2,1,0:T(2,128)(2,1)S(1)} %get-tuple-element.247), channel_id=1, source_target_pairs={{4,0},{8,4},{12,8},{0,12},{5,1},{9,5},{13,9},{1,13},{6,2},{10,6},{... | collective-permute-start | bytes 49160 | tf_op jit(solution)/shard_map/ppermute | solution.py:25
  155.1 2.1 collective-permute-start.22
  157.3 4.3 %collective-permute-done.22 = bf16[2,32,10,1]{3,2,1,0:T(8,128)(2,1)S(1)} collective-permute-done((bf16[2,32,10,1]{3,2,1,0:T(8,128)(2,1)S(1)}, bf16[2,32,10,1]{3,2,1,0:T(8,128)(2,1)S(1)}, u32[]{:S(2)}, u32[]{:S(2)}) %collective-permute-start.22) | collective-permute-done | bytes 1312 | tf_op jit(solution)/shard_map/ppermute | solution.py:22
  161.6 2.8 %collective-permute-done.23 = bf16[2,32,10,1]{3,2,1,0:T(8,128)(2,1)S(1)} collective-permute-done((bf16[2,32,10,1]{3,2,1,0:T(8,128)(2,1)S(1)}, bf16[2,32,10,1]{3,2,1,0:T(8,128)(2,1)S(1)}, u32[]{:S(2)}, u32[]{:S(2)}) %collective-permute-start.23) | collective-permute-done | bytes 1312 | tf_op jit(solution)/shard_map/ppermute | solution.py:25
  165.0 2.7 %conditional.17 = (bf16[2,136,8,128]{3,1,2,0:T(8,128)(2,1)S(1)}) conditional(s32[]{:T(128)} %convert_element_type.72, (pred[130]{0:T(512)(128)(4,1)}, bf16[2,32,10,130]{3,2,1,0:T(8,128)(2,1)S(1)}, bf16[2,32,10,130]{3,1,2,0:T(8,128)(2,1)S(1)}, bf16[3,3,32,136]{3,2,1,0:T(8,128)(2,1)}) %tuple.84, () %tuple.85), branch_computations={%region_16.17_spmd, %region_17.18_spmd} | conditional | flops 163022080 | bytes 4987046 | solution.py:148
  171.3 2.7 %collective-permute-start.25 = (bf16[2,136,2,128]{1,3,2,0:T(8,128)(2,1)S(1)}, bf16[2,136,2,128]{1,3,2,0:T(8,128)(2,1)S(1)}, u32[]{:S(2)}, u32[]{:S(2)}) collective-permute-start(bf16[2,136,2,128]{1,3,2,0:T(8,128)(2,1)S(1)} %get-tuple-element.233), channel_id=1, source_target_pairs={{4,0},{8,4},{12,8},{0,12},{5,1},{9,5},{13,9},{1,13},{6,2},{10,6},{... | collective-permute-start | bytes 417800 | tf_op jit(solution)/shard_map/ppermute | solution.py:25
  174.0 4.4 %collective-permute-done.24 = bf16[2,136,2,128]{1,3,2,0:T(8,128)(2,1)S(1)} collective-permute-done((bf16[2,136,2,128]{1,3,2,0:T(8,128)(2,1)S(1)}, bf16[2,136,2,128]{1,3,2,0:T(8,128)(2,1)S(1)}, u32[]{:S(2)}, u32[]{:S(2)}) %collective-permute-start.24) | collective-permute-done | bytes 139296 | tf_op jit(solution)/shard_map/ppermute | solution.py:22
  178.4 2.1 collective-permute-done.25
  186.6 9.4 %conditional.18 = (bf16[2,136,8,128]{3,1,2,0:T(8,128)(2,1)S(1)}) conditional(s32[]{:T(128)} %convert_element_type.72, (pred[132]{0:T(512)(128)(4,1)S(1)}, bf16[2,136,12,132]{1,3,2,0:T(8,128)(2,1)}, bf16[2,136,12,132]{3,1,2,0:T(8,128)(2,1)}, bf16[3,3,136,136]{3,2,1,0:T(8,128)(2,1)}) %tuple.164, () %tuple.87), branch_computations={%region_18.19_spmd, %region_19.20_spmd} | conditional | flops 684774144 | bytes 21570856 | solution.py:148
  186.6 3.8 %copy.83 = bf16[2,136,12,132]{3,1,2,0:T(8,128)(2,1)} copy(bf16[2,136,12,132]{1,3,2,0:T(8,128)(2,1)} %get-tuple-element.210) | data formatting | bytes 1723392 | tf_op jit(solution)/shard_map
  190.4 2.1 broadcast_select_fusion.3
  200.2 2.7 %collective-permute-start.29 = (bf16[2,136,4,128]{1,2,3,0:T(4,128)(2,1)S(1)}, bf16[2,136,4,128]{1,2,3,0:T(4,128)(2,1)S(1)}, u32[]{:S(2)}, u32[]{:S(2)}) collective-permute-start(bf16[2,136,4,128]{1,2,3,0:T(4,128)(2,1)S(1)} %get-tuple-element.231), channel_id=1, source_target_pairs={{4,0},{8,4},{12,8},{0,12},{5,1},{9,5},{13,9},{1,13},{6,2},{10,6},{... | collective-permute-start | bytes 835592 | tf_op jit(solution)/shard_map/ppermute | solution.py:25
  202.8 7.3 %collective-permute-done.28 = bf16[2,136,4,128]{1,2,3,0:T(4,128)(2,1)S(1)} collective-permute-done((bf16[2,136,4,128]{1,2,3,0:T(4,128)(2,1)S(1)}, bf16[2,136,4,128]{1,2,3,0:T(4,128)(2,1)S(1)}, u32[]{:S(2)}, u32[]{:S(2)}) %collective-permute-start.28) | collective-permute-done | bytes 278560 | tf_op jit(solution)/shard_map/ppermute | solution.py:22
  210.1 4.9 %collective-permute-done.29 = bf16[2,136,4,128]{1,2,3,0:T(4,128)(2,1)S(1)} collective-permute-done((bf16[2,136,4,128]{1,2,3,0:T(4,128)(2,1)S(1)}, bf16[2,136,4,128]{1,2,3,0:T(4,128)(2,1)S(1)}, u32[]{:S(2)}, u32[]{:S(2)}) %collective-permute-start.29) | collective-permute-done | bytes 278560 | tf_op jit(solution)/shard_map/ppermute | solution.py:25
  217.1 2.2 collective-permute-done.30
  220.1 2.6 %pad_maximum_fusion.1 = bf16[2,136,16,136]{1,2,3,0:T(8,128)(2,1)} fusion(bf16[2,136,16,4]{1,2,3,0:T(8,128)(2,1)S(1)} %collective-permute-done.31, bf16[2,136,4,128]{1,2,3,0:T(4,128)(2,1)S(1)} %collective-permute-done.29, bf16[2,136,8,128]{1,2,3,0:T(8,128)(2,1)S(1)} %copy.84, bf16[2,136,4,128]{1,2,3,0:T(4,128)(2,1)S(1)} %collective-permute-done.28, ...), kind=kLoop, calls=%fused_computation.189 | loop fusion | flops 5918720 | bytes 2367488 | tf_op jit(solution)/shard_map/concatenate | solution.py:26
  222.7 14.7 %conditional.19 = (f32[2,24,8,128]{3,2,1,0:T(8,128)S(1)}) conditional(s32[]{:T(128)} %convert_element_type.72, (pred[136]{0:T(512)(128)(4,1)S(1)}, bf16[2,136,16,136]{1,2,3,0:T(8,128)(2,1)}, bf16[2,136,16,136]{3,1,2,0:T(8,128)(2,1)S(1)}, bf16[3,3,136,32]{2,3,1,0:T(8,128)(2,1)S(1)}) %tuple.163, () %tuple.89), branch_computations={%region_20.21_spmd, %region_21.22_spmd} | conditional | flops 161024000 | bytes 42453676 | solution.py:148
  222.7 4.6 %copy.87 = bf16[2,136,16,136]{3,1,2,0:T(8,128)(2,1)} copy(bf16[2,136,16,136]{1,2,3,0:T(8,128)(2,1)} %get-tuple-element.214) | data formatting | bytes 2367488 | tf_op jit(solution)/shard_map
  231.4 2.3 copy-done.3
  233.9 3.3 %convolution_bitcast_fusion.9 = f32[2,32,8,128]{3,1,2,0:T(8,128)S(1)} fusion(bf16[2,1224,8,128]{3,1,2,0:T(8,128)(2,1)} %copy-done.3, bf16[1224,32,1,1]{0,1,2,3:T(8,128)(2,1)S(1)} %reshape.67), kind=kOutput, calls=%fused_computation.177 | convolution fusion | flops 160432128 | bytes 5353984 | tf_op jit(solution)/shard_map/cond/branch_0_fun/mkrc,ko->morc/dot_general | solution.py:50
  (210 shorter events, 78.6 us)
Async XLA Ops:
  2.2 6.8 %collective-permute-start = (bf16[2,16,1,128]{3,1,2,0:T(8,128)(2,1)S(1)}, bf16[2,16,1,128]{3,1,2,0:T(8,128)(2,1)S(1)}, u32[]{:S(2)}, u32[]{:S(2)}) collective-permute-start(bf16[2,16,1,128]{3,1,2,0:T(8,128)(2,1)S(1)} %get-tuple-element.252), channel_id=1, source_target_pairs={{0,4},{4,8},{8,12},{12,0},{1,5},{5,9},{9,13},{13,1},{2,6},{6,10},{... | collective-permute-start | bytes 24584 | tf_op jit(solution)/shard_map/ppermute | solution.py:22
  5.3 3.7 %collective-permute-start.1 = (bf16[2,16,1,128]{3,1,2,0:T(8,128)(2,1)S(1)}, bf16[2,16,1,128]{3,1,2,0:T(8,128)(2,1)S(1)}, u32[]{:S(2)}, u32[]{:S(2)}) collective-permute-start(bf16[2,16,1,128]{3,1,2,0:T(8,128)(2,1)S(1)} %get-tuple-element.253), channel_id=1, source_target_pairs={{4,0},{8,4},{12,8},{0,12},{5,1},{9,5},{13,9},{1,13},{6,2},{10,6},{... | collective-permute-start | bytes 24584 | tf_op jit(solution)/shard_map/ppermute | solution.py:25
  9.0 4.1 %copy-start.8 = (bf16[2,24,8,128]{3,2,1,0:T(8,128)(2,1)S(1)}, bf16[2,24,8,128]{3,2,1,0:T(8,128)(2,1)}, u32[]{:S(2)}) copy-start(bf16[2,24,8,128]{3,2,1,0:T(8,128)(2,1)} %param.29) | copy-start | bytes 294916
  9.1 4.1 %copy-start.16 = (s32[8,128]{1,0:T(8,128)S(1)}, s32[8,128]{1,0:T(8,128)}, u32[]{:S(2)}) copy-start(s32[8,128]{1,0:T(8,128)} %param.32) | copy-start | bytes 12292
  9.1 6.8 %copy-start.10 = (bf16[3,3,136,8]{2,3,1,0:T(8,128)(2,1)S(1)}, bf16[3,3,136,8]{2,3,1,0:T(8,128)(2,1)}, u32[]{:S(2)}) copy-start(bf16[3,3,136,8]{2,3,1,0:T(8,128)(2,1)} %param.37) | copy-start | bytes 58756
  9.2 6.4 %collective-permute-start.2 = (bf16[2,136,1,128]{3,1,2,0:T(8,128)(2,1)S(1)}, bf16[2,136,1,128]{3,1,2,0:T(8,128)(2,1)S(1)}, u32[]{:S(2)}, u32[]{:S(2)}) collective-permute-start(bf16[2,136,1,128]{3,1,2,0:T(8,128)(2,1)S(1)} %get-tuple-element.240), channel_id=1, source_target_pairs={{0,4},{4,8},{8,12},{12,0},{1,5},{5,9},{9,13},{13,1},{2,6},{6,10},{... | collective-permute-start | bytes 208904 | tf_op jit(solution)/shard_map/ppermute | solution.py:22
  10.7 5.1 %collective-permute-start.3 = (bf16[2,136,1,128]{3,1,2,0:T(8,128)(2,1)S(1)}, bf16[2,136,1,128]{3,1,2,0:T(8,128)(2,1)S(1)}, u32[]{:S(2)}, u32[]{:S(2)}) collective-permute-start(bf16[2,136,1,128]{3,1,2,0:T(8,128)(2,1)S(1)} %get-tuple-element.241), channel_id=1, source_target_pairs={{4,0},{8,4},{12,8},{0,12},{5,1},{9,5},{13,9},{1,13},{6,2},{10,6},{... | collective-permute-start | bytes 208904 | tf_op jit(solution)/shard_map/ppermute | solution.py:25
  13.2 2.8 %copy-start.14 = (f32[8,128]{1,0:T(8,128)}, f32[8,128]{1,0:T(8,128)S(1)}, u32[]{:S(2)}) copy-start(f32[8,128]{1,0:T(8,128)S(1)} %convert_element_type.74) | copy-start | bytes 12292
  15.9 27.4 %copy-start.23 = (bf16[3,3,32,136]{3,2,1,0:T(8,128)(2,1)S(1)}, bf16[3,3,32,136]{3,2,1,0:T(8,128)(2,1)}, u32[]{:S(2)}) copy-start(bf16[3,3,32,136]{3,2,1,0:T(8,128)(2,1)} %param.33) | copy-start | bytes 235012
  29.9 5.6 %collective-permute-start.4 = (bf16[2,32,1,128]{3,1,2,0:T(8,128)(2,1)S(1)}, bf16[2,32,1,128]{3,1,2,0:T(8,128)(2,1)S(1)}, u32[]{:S(2)}, u32[]{:S(2)}) collective-permute-start(bf16[2,32,1,128]{3,1,2,0:T(8,128)(2,1)S(1)} %get-tuple-element.248), channel_id=1, source_target_pairs={{0,4},{4,8},{8,12},{12,0},{1,5},{5,9},{9,13},{13,1},{2,6},{6,10},{... | collective-permute-start | bytes 49160 | tf_op jit(solution)/shard_map/ppermute | solution.py:22
  31.0 4.5 %collective-permute-start.5 = (bf16[2,32,1,128]{3,1,2,0:T(8,128)(2,1)S(1)}, bf16[2,32,1,128]{3,1,2,0:T(8,128)(2,1)S(1)}, u32[]{:S(2)}, u32[]{:S(2)}) collective-permute-start(bf16[2,32,1,128]{3,1,2,0:T(8,128)(2,1)S(1)} %get-tuple-element.249), channel_id=1, source_target_pairs={{4,0},{8,4},{12,8},{0,12},{5,1},{9,5},{13,9},{1,13},{6,2},{10,6},{... | collective-permute-start | bytes 49160 | tf_op jit(solution)/shard_map/ppermute | solution.py:25
  35.7 5.4 %collective-permute-start.6 = (bf16[2,32,10,1]{3,1,2,0:T(8,128)(2,1)S(1)}, bf16[2,32,10,1]{3,1,2,0:T(8,128)(2,1)S(1)}, u32[]{:S(2)}, u32[]{:S(2)}) collective-permute-start(bf16[2,32,10,1]{3,1,2,0:T(8,128)(2,1)S(1)} %get-tuple-element.244), channel_id=1, source_target_pairs={{0,2},{2,0},{1,3},{3,1},{4,6},{6,4},{5,7},{7,5},{8,10},{10,8},{9,1... | collective-permute-start | bytes 3848 | tf_op jit(solution)/shard_map/ppermute | solution.py:22
  37.8 5.3 %collective-permute-start.7 = (bf16[2,32,10,1]{3,1,2,0:T(8,128)(2,1)S(1)}, bf16[2,32,10,1]{3,1,2,0:T(8,128)(2,1)S(1)}, u32[]{:S(2)}, u32[]{:S(2)}) collective-permute-start(bf16[2,32,10,1]{3,1,2,0:T(8,128)(2,1)S(1)} %get-tuple-element.245), channel_id=1, source_target_pairs={{2,0},{0,2},{3,1},{1,3},{6,4},{4,6},{7,5},{5,7},{10,8},{8,10},{11,... | collective-permute-start | bytes 3848 | tf_op jit(solution)/shard_map/ppermute | solution.py:25
  46.2 8.3 %collective-permute-start.8 = (bf16[2,136,2,128]{1,3,2,0:T(8,128)(2,1)S(1)}, bf16[2,136,2,128]{1,3,2,0:T(8,128)(2,1)S(1)}, u32[]{:S(2)}, u32[]{:S(2)}) collective-permute-start(bf16[2,136,2,128]{1,3,2,0:T(8,128)(2,1)S(1)} %get-tuple-element.236), channel_id=1, source_target_pairs={{0,4},{4,8},{8,12},{12,0},{1,5},{5,9},{9,13},{13,1},{2,6},{6,10},{... | collective-permute-start | bytes 417800 | tf_op jit(solution)/shard_map/ppermute | solution.py:22
  47.3 9.2 %collective-permute-start.9 = (bf16[2,136,2,128]{1,3,2,0:T(8,128)(2,1)S(1)}, bf16[2,136,2,128]{1,3,2,0:T(8,128)(2,1)S(1)}, u32[]{:S(2)}, u32[]{:S(2)}) collective-permute-start(bf16[2,136,2,128]{1,3,2,0:T(8,128)(2,1)S(1)} %get-tuple-element.237), channel_id=1, source_target_pairs={{4,0},{8,4},{12,8},{0,12},{5,1},{9,5},{13,9},{1,13},{6,2},{10,6},{... | collective-permute-start | bytes 417800 | tf_op jit(solution)/shard_map/ppermute | solution.py:25
  56.5 3.9 %copy-start.4 = (bf16[2,136,2,128]{1,3,2,0:T(8,128)(2,1)}, bf16[2,136,2,128]{1,3,2,0:T(8,128)(2,1)S(1)}, u32[]{:S(2)}) copy-start(bf16[2,136,2,128]{1,3,2,0:T(8,128)(2,1)S(1)} %collective-permute-done.9) | copy-start | bytes 417796
  56.6 3.9 %collective-permute-start.10 = (bf16[2,136,12,2]{1,3,2,0:T(2,128)(2,1)S(1)}, bf16[2,136,12,2]{1,3,2,0:T(2,128)(2,1)S(1)}, u32[]{:S(2)}, u32[]{:S(2)}) collective-permute-start(bf16[2,136,12,2]{1,3,2,0:T(2,128)(2,1)S(1)} %get-tuple-element.228), channel_id=1, source_target_pairs={{0,2},{2,0},{1,3},{3,1},{4,6},{6,4},{5,7},{7,5},{8,10},{10,8},{9,1... | collective-permute-start | bytes 39176 | tf_op jit(solution)/shard_map/ppermute | solution.py:22
  56.7 4.1 %collective-permute-start.11 = (bf16[2,136,12,2]{1,3,2,0:T(2,128)(2,1)S(1)}, bf16[2,136,12,2]{1,3,2,0:T(2,128)(2,1)S(1)}, u32[]{:S(2)}, u32[]{:S(2)}) collective-permute-start(bf16[2,136,12,2]{1,3,2,0:T(2,128)(2,1)S(1)} %get-tuple-element.229), channel_id=1, source_target_pairs={{2,0},{0,2},{3,1},{1,3},{6,4},{4,6},{7,5},{5,7},{10,8},{8,10},{11,... | collective-permute-start | bytes 39176 | tf_op jit(solution)/shard_map/ppermute | solution.py:25
  58.7 5.1 %copy-start.19 = (pred[132]{0:T(512)(128)(4,1)}, pred[132]{0:T(512)(128)(4,1)S(1)}, u32[]{:S(2)}) copy-start(pred[132]{0:T(512)(128)(4,1)S(1)} %compare_and_fusion.1) | copy-start | bytes 400
  73.9 13.9 %collective-permute-start.12 = (bf16[2,136,4,128]{1,2,3,0:T(4,128)(2,1)}, bf16[2,136,4,128]{1,2,3,0:T(4,128)(2,1)S(1)}, u32[]{:S(2)}, u32[]{:S(2)}) collective-permute-start(bf16[2,136,4,128]{1,2,3,0:T(4,128)(2,1)} %get-tuple-element.234), channel_id=1, source_target_pairs={{0,4},{4,8},{8,12},{12,0},{1,5},{5,9},{9,13},{13,1},{2,6},{6,10},{... | collective-permute-start | bytes 835592 | tf_op jit(solution)/shard_map/ppermute | solution.py:22
  75.2 17.9 %collective-permute-start.13 = (bf16[2,136,4,128]{1,2,3,0:T(4,128)(2,1)S(1)}, bf16[2,136,4,128]{1,2,3,0:T(4,128)(2,1)S(1)}, u32[]{:S(2)}, u32[]{:S(2)}) collective-permute-start(bf16[2,136,4,128]{1,2,3,0:T(4,128)(2,1)S(1)} %get-tuple-element.235), channel_id=1, source_target_pairs={{4,0},{8,4},{12,8},{0,12},{5,1},{9,5},{13,9},{1,13},{6,2},{10,6},{... | collective-permute-start | bytes 835592 | tf_op jit(solution)/shard_map/ppermute | solution.py:25
  93.2 4.3 %collective-permute-start.14 = (bf16[2,136,16,4]{1,2,3,0:T(8,128)(2,1)S(1)}, bf16[2,136,16,4]{1,2,3,0:T(8,128)(2,1)S(1)}, u32[]{:S(2)}, u32[]{:S(2)}) collective-permute-start(bf16[2,136,16,4]{1,2,3,0:T(8,128)(2,1)S(1)} %get-tuple-element.224), channel_id=1, source_target_pairs={{0,2},{2,0},{1,3},{3,1},{4,6},{6,4},{5,7},{7,5},{8,10},{10,8},{9,1... | collective-permute-start | bytes 104456 | tf_op jit(solution)/shard_map/ppermute | solution.py:22
  93.3 5.0 %collective-permute-start.15 = (bf16[2,136,16,4]{1,2,3,0:T(8,128)(2,1)S(1)}, bf16[2,136,16,4]{1,2,3,0:T(8,128)(2,1)S(1)}, u32[]{:S(2)}, u32[]{:S(2)}) collective-permute-start(bf16[2,136,16,4]{1,2,3,0:T(8,128)(2,1)S(1)} %get-tuple-element.225), channel_id=1, source_target_pairs={{2,0},{0,2},{3,1},{1,3},{6,4},{4,6},{7,5},{5,7},{10,8},{8,10},{11,... | collective-permute-start | bytes 104456 | tf_op jit(solution)/shard_map/ppermute | solution.py:25
  95.3 6.5 %copy-start.17 = (pred[136]{0:T(512)(128)(4,1)}, pred[136]{0:T(512)(128)(4,1)S(1)}, u32[]{:S(2)}) copy-start(pred[136]{0:T(512)(128)(4,1)S(1)} %compare_and_fusion.2) | copy-start | bytes 412
  110.4 2.3 copy-start.2
  121.2 5.6 %collective-permute-start.16 = (bf16[2,16,1,128]{3,2,1,0:T(2,128)(2,1)S(1)}, bf16[2,16,1,128]{3,2,1,0:T(2,128)(2,1)S(1)}, u32[]{:S(2)}, u32[]{:S(2)}) collective-permute-start(bf16[2,16,1,128]{3,2,1,0:T(2,128)(2,1)S(1)} %get-tuple-element.250), channel_id=1, source_target_pairs={{0,4},{4,8},{8,12},{12,0},{1,5},{5,9},{9,13},{13,1},{2,6},{6,10},{... | collective-permute-start | bytes 24584 | tf_op jit(solution)/shard_map/ppermute | solution.py:22
  121.6 5.2 %collective-permute-start.17 = (bf16[2,16,1,128]{3,2,1,0:T(2,128)(2,1)S(1)}, bf16[2,16,1,128]{3,2,1,0:T(2,128)(2,1)S(1)}, u32[]{:S(2)}, u32[]{:S(2)}) collective-permute-start(bf16[2,16,1,128]{3,2,1,0:T(2,128)(2,1)S(1)} %get-tuple-element.251), channel_id=1, source_target_pairs={{4,0},{8,4},{12,8},{0,12},{5,1},{9,5},{13,9},{1,13},{6,2},{10,6},{... | collective-permute-start | bytes 24584 | tf_op jit(solution)/shard_map/ppermute | solution.py:25
  126.9 5.8 %copy-start.9 = (bf16[2,24,8,128]{3,2,1,0:T(8,128)(2,1)S(1)}, bf16[2,24,8,128]{3,2,1,0:T(8,128)(2,1)}, u32[]{:S(2)}) copy-start(bf16[2,24,8,128]{3,2,1,0:T(8,128)(2,1)} %param.29) | copy-start | bytes 294916
  126.9 9.2 %copy-start.11 = (bf16[3,3,136,8]{2,3,1,0:T(8,128)(2,1)S(1)}, bf16[3,3,136,8]{2,3,1,0:T(8,128)(2,1)}, u32[]{:S(2)}) copy-start(bf16[3,3,136,8]{2,3,1,0:T(8,128)(2,1)} %param.37) | copy-start | bytes 58756
  128.7 6.2 %collective-permute-start.18 = (bf16[2,136,1,128]{3,1,2,0:T(8,128)(2,1)S(1)}, bf16[2,136,1,128]{3,1,2,0:T(8,128)(2,1)S(1)}, u32[]{:S(2)}, u32[]{:S(2)}) collective-permute-start(bf16[2,136,1,128]{3,1,2,0:T(8,128)(2,1)S(1)} %get-tuple-element.238), channel_id=1, source_target_pairs={{0,4},{4,8},{8,12},{12,0},{1,5},{5,9},{9,13},{13,1},{2,6},{6,10},{... | collective-permute-start | bytes 208904 | tf_op jit(solution)/shard_map/ppermute | solution.py:22
  128.8 6.1 %collective-permute-start.19 = (bf16[2,136,1,128]{3,1,2,0:T(8,128)(2,1)S(1)}, bf16[2,136,1,128]{3,1,2,0:T(8,128)(2,1)S(1)}, u32[]{:S(2)}, u32[]{:S(2)}) collective-permute-start(bf16[2,136,1,128]{3,1,2,0:T(8,128)(2,1)S(1)} %get-tuple-element.239), channel_id=1, source_target_pairs={{4,0},{8,4},{12,8},{0,12},{5,1},{9,5},{13,9},{1,13},{6,2},{10,6},{... | collective-permute-start | bytes 208904 | tf_op jit(solution)/shard_map/ppermute | solution.py:25
  148.7 16.4 %copy-start.12 = (bf16[2,8,8,128]{3,2,1,0:T(8,128)(2,1)}, bf16[2,8,8,128]{3,2,1,0:T(8,128)(2,1)S(1)}, u32[]{:S(2)}) copy-start(bf16[2,8,8,128]{3,2,1,0:T(8,128)(2,1)S(1)} %reduce_sum.25) | copy-start | bytes 98308
  148.7 6.1 %collective-permute-start.20 = (bf16[2,32,1,128]{3,2,1,0:T(2,128)(2,1)S(1)}, bf16[2,32,1,128]{3,2,1,0:T(2,128)(2,1)S(1)}, u32[]{:S(2)}, u32[]{:S(2)}) collective-permute-start(bf16[2,32,1,128]{3,2,1,0:T(2,128)(2,1)S(1)} %get-tuple-element.246), channel_id=1, source_target_pairs={{0,4},{4,8},{8,12},{12,0},{1,5},{5,9},{9,13},{13,1},{2,6},{6,10},{... | collective-permute-start | bytes 49160 | tf_op jit(solution)/shard_map/ppermute | solution.py:22
  150.4 4.4 %collective-permute-start.21 = (bf16[2,32,1,128]{3,2,1,0:T(2,128)(2,1)S(1)}, bf16[2,32,1,128]{3,2,1,0:T(2,128)(2,1)S(1)}, u32[]{:S(2)}, u32[]{:S(2)}) collective-permute-start(bf16[2,32,1,128]{3,2,1,0:T(2,128)(2,1)S(1)} %get-tuple-element.247), channel_id=1, source_target_pairs={{4,0},{8,4},{12,8},{0,12},{5,1},{9,5},{13,9},{1,13},{6,2},{10,6},{... | collective-permute-start | bytes 49160 | tf_op jit(solution)/shard_map/ppermute | solution.py:25
  155.1 6.5 %collective-permute-start.22 = (bf16[2,32,10,1]{3,2,1,0:T(8,128)(2,1)S(1)}, bf16[2,32,10,1]{3,2,1,0:T(8,128)(2,1)S(1)}, u32[]{:S(2)}, u32[]{:S(2)}) collective-permute-start(bf16[2,32,10,1]{3,2,1,0:T(8,128)(2,1)S(1)} %get-tuple-element.242), channel_id=1, source_target_pairs={{0,2},{2,0},{1,3},{3,1},{4,6},{6,4},{5,7},{7,5},{8,10},{10,8},{9,1... | collective-permute-start | bytes 3848 | tf_op jit(solution)/shard_map/ppermute | solution.py:22
  157.3 7.2 %collective-permute-start.23 = (bf16[2,32,10,1]{3,2,1,0:T(8,128)(2,1)S(1)}, bf16[2,32,10,1]{3,2,1,0:T(8,128)(2,1)S(1)}, u32[]{:S(2)}, u32[]{:S(2)}) collective-permute-start(bf16[2,32,10,1]{3,2,1,0:T(8,128)(2,1)S(1)} %get-tuple-element.243), channel_id=1, source_target_pairs={{2,0},{0,2},{3,1},{1,3},{6,4},{4,6},{7,5},{5,7},{10,8},{8,10},{11,... | collective-permute-start | bytes 3848 | tf_op jit(solution)/shard_map/ppermute | solution.py:25
  165.3 1.7 copy-start.24
  170.0 8.4 %collective-permute-start.24 = (bf16[2,136,2,128]{1,3,2,0:T(8,128)(2,1)S(1)}, bf16[2,136,2,128]{1,3,2,0:T(8,128)(2,1)S(1)}, u32[]{:S(2)}, u32[]{:S(2)}) collective-permute-start(bf16[2,136,2,128]{1,3,2,0:T(8,128)(2,1)S(1)} %get-tuple-element.232), channel_id=1, source_target_pairs={{0,4},{4,8},{8,12},{12,0},{1,5},{5,9},{9,13},{13,1},{2,6},{6,10},{... | collective-permute-start | bytes 417800 | tf_op jit(solution)/shard_map/ppermute | solution.py:22
  171.3 15.3 %copy-start.20 = (pred[132]{0:T(512)(128)(4,1)S(1)}, pred[132]{0:T(512)(128)(4,1)}, u32[]{:S(2)}) copy-start(pred[132]{0:T(512)(128)(4,1)} %copy-done.19) | copy-start | bytes 400
  171.3 9.2 %collective-permute-start.25 = (bf16[2,136,2,128]{1,3,2,0:T(8,128)(2,1)S(1)}, bf16[2,136,2,128]{1,3,2,0:T(8,128)(2,1)S(1)}, u32[]{:S(2)}, u32[]{:S(2)}) collective-permute-start(bf16[2,136,2,128]{1,3,2,0:T(8,128)(2,1)S(1)} %get-tuple-element.233), channel_id=1, source_target_pairs={{4,0},{8,4},{12,8},{0,12},{5,1},{9,5},{13,9},{1,13},{6,2},{10,6},{... | collective-permute-start | bytes 417800 | tf_op jit(solution)/shard_map/ppermute | solution.py:25
  180.6 3.9 %collective-permute-start.26 = (bf16[2,136,12,2]{1,3,2,0:T(2,128)(2,1)S(1)}, bf16[2,136,12,2]{1,3,2,0:T(2,128)(2,1)S(1)}, u32[]{:S(2)}, u32[]{:S(2)}) collective-permute-start(bf16[2,136,12,2]{1,3,2,0:T(2,128)(2,1)S(1)} %get-tuple-element.226), channel_id=1, source_target_pairs={{0,2},{2,0},{1,3},{3,1},{4,6},{6,4},{5,7},{7,5},{8,10},{10,8},{9,1... | collective-permute-start | bytes 39176 | tf_op jit(solution)/shard_map/ppermute | solution.py:22
  180.6 4.1 %collective-permute-start.27 = (bf16[2,136,12,2]{1,3,2,0:T(2,128)(2,1)S(1)}, bf16[2,136,12,2]{1,3,2,0:T(2,128)(2,1)S(1)}, u32[]{:S(2)}, u32[]{:S(2)}) collective-permute-start(bf16[2,136,12,2]{1,3,2,0:T(2,128)(2,1)S(1)} %get-tuple-element.227), channel_id=1, source_target_pairs={{2,0},{0,2},{3,1},{1,3},{6,4},{4,6},{7,5},{5,7},{10,8},{8,10},{11,... | collective-permute-start | bytes 39176 | tf_op jit(solution)/shard_map/ppermute | solution.py:25
  199.0 11.1 %collective-permute-start.28 = (bf16[2,136,4,128]{1,2,3,0:T(4,128)(2,1)S(1)}, bf16[2,136,4,128]{1,2,3,0:T(4,128)(2,1)S(1)}, u32[]{:S(2)}, u32[]{:S(2)}) collective-permute-start(bf16[2,136,4,128]{1,2,3,0:T(4,128)(2,1)S(1)} %get-tuple-element.230), channel_id=1, source_target_pairs={{0,4},{4,8},{8,12},{12,0},{1,5},{5,9},{9,13},{13,1},{2,6},{6,10},{... | collective-permute-start | bytes 835592 | tf_op jit(solution)/shard_map/ppermute | solution.py:22
  200.2 14.8 %collective-permute-start.29 = (bf16[2,136,4,128]{1,2,3,0:T(4,128)(2,1)S(1)}, bf16[2,136,4,128]{1,2,3,0:T(4,128)(2,1)S(1)}, u32[]{:S(2)}, u32[]{:S(2)}) collective-permute-start(bf16[2,136,4,128]{1,2,3,0:T(4,128)(2,1)S(1)} %get-tuple-element.231), channel_id=1, source_target_pairs={{4,0},{8,4},{12,8},{0,12},{5,1},{9,5},{13,9},{1,13},{6,2},{10,6},{... | collective-permute-start | bytes 835592 | tf_op jit(solution)/shard_map/ppermute | solution.py:25
  215.0 4.3 %collective-permute-start.30 = (bf16[2,136,16,4]{1,2,3,0:T(8,128)(2,1)S(1)}, bf16[2,136,16,4]{1,2,3,0:T(8,128)(2,1)S(1)}, u32[]{:S(2)}, u32[]{:S(2)}) collective-permute-start(bf16[2,136,16,4]{1,2,3,0:T(8,128)(2,1)S(1)} %get-tuple-element.222), channel_id=1, source_target_pairs={{0,2},{2,0},{1,3},{3,1},{4,6},{6,4},{5,7},{7,5},{8,10},{10,8},{9,1... | collective-permute-start | bytes 104456 | tf_op jit(solution)/shard_map/ppermute | solution.py:22
  215.1 5.0 %collective-permute-start.31 = (bf16[2,136,16,4]{1,2,3,0:T(8,128)(2,1)S(1)}, bf16[2,136,16,4]{1,2,3,0:T(8,128)(2,1)S(1)}, u32[]{:S(2)}, u32[]{:S(2)}) collective-permute-start(bf16[2,136,16,4]{1,2,3,0:T(8,128)(2,1)S(1)} %get-tuple-element.223), channel_id=1, source_target_pairs={{2,0},{0,2},{3,1},{1,3},{6,4},{4,6},{7,5},{5,7},{10,8},{8,10},{11,... | collective-permute-start | bytes 104456 | tf_op jit(solution)/shard_map/ppermute | solution.py:25
  217.1 5.6 %copy-start.18 = (pred[136]{0:T(512)(128)(4,1)S(1)}, pred[136]{0:T(512)(128)(4,1)}, u32[]{:S(2)}) copy-start(pred[136]{0:T(512)(128)(4,1)} %copy-done.17) | copy-start | bytes 412
  231.3 2.3 copy-start.3
  (7 other events, 6.2 us)
